TPU v7x, 32 devices: a whole 2x2x4 slice. The times are simulated.
32 devices in a mesh: groups: 2 (over y), space: 4 (over z), tm: 2 (over x), chan: 2 (over core).
Axes of the slice: x: 2, y: 2, z: 4, core: 2. Of those that a mesh axis runs over, the one named last changes fastest.
Arguments:
- features: float32 [48, 40, 384], P(('groups', 'space'), 'tm'), parts along dimension 0, may hold values from -50 to 50
- norm1_gain: float32 [384], replicated, may hold values from 0.25 to 1.75
- norm1_shift: float32 [384], replicated, may hold values from -3 to 3
- conv1_weight: float32 [3, 3, 384, 384], P(None, None, 'space', 'chan'), may hold values from -0.109375 to 0.109375
- norm2_gain: float32 [384], replicated, may hold values from 0.25 to 1.75
- norm2_shift: float32 [384], replicated, may hold values from -3 to 3
- conv2_weight: float32 [3, 3, 384, 384], P(None, None, 'space', 'chan'), may hold values from -0.109375 to 0.109375
- head_gain: float32 [384], replicated, may hold values from 0.25 to 1.75
- head_shift: float32 [384], replicated, may hold values from -3 to 3
- head_weight: float32 [3, 3, 384, 16], P(None, None, 'space', 'chan'), may hold values from -0.109375 to 0.109375
- head_bias: float32 [16], P('chan'), may hold values from -3 to 3
- noisy_latents: float32 [4, 16, 24, 40], P(('groups', 'tm'), None, 'space'), parts along dimension 0, may hold values from -6 to 6
- later_cond: float32 [4, 16, 24, 40], P(('groups', 'tm'), None, 'space'), parts along dimension 0, may hold values from -6 to 6
- patch_weight: float32 [144, 5120], P(None, 'chan'), may hold values from -0.5 to 0.5
- patch_bias: float32 [5120], P('chan'), may hold values from -3 to 3
Outputs:
- tokens: float32 [4, 12, 20, 5120], P(('groups', 'tm'), 'space', None, 'chan'), parts along dimension 0
- image_latent: float32 [48, 40, 16], P(('groups', 'space'), 'tm'), parts along dimension 0
There are 2 independent parts, one for each index of `groups`. A program takes and returns all parts, laid end to end along the dimension named above; an argument that names none is the same for every part. Nothing has to cross between parts.
All inputs are finite; a program needn't handle non-finite values.
Results may differ from a plain program's by a relative error of at most 0.00007.
Values sent between devices are 32-bit elements; how exact they have to be, the bound alone decides.
A program may use at most 64 MiB of HBM per device.

v0:
```python
import jax
import jax.numpy as jnp
from jax import lax
from jax.sharding import PartitionSpec as P

NGROUP = 32


EPSILON = 1e-06
HIGHEST = lax.Precision.HIGHEST


def padded_2(cells, sides, width):
    for axis, dim in sides:
        count = lax.axis_size(axis)
        ends = count - 1
        head = lax.slice_in_dim(cells, 0, width, axis=dim)
        tail = lax.slice_in_dim(cells, cells.shape[dim] - width, cells.shape[dim], axis=dim)
        cells = jnp.concatenate(
            [
                lax.ppermute(tail, axis, [(i, (i + 1) % count) for i in range(ends)]),
                cells,
                lax.ppermute(head, axis, [((i + 1) % count, i) for i in range(ends)]),
            ],
            axis=dim,
        )
    return cells


def group_stats(inner, count_all):
    grouped = inner.reshape(-1, NGROUP, inner.shape[-1] // NGROUP)
    totals, squares = lax.psum(
        (jnp.sum(grouped, axis=(0, 2)), jnp.sum(grouped * grouped, axis=(0, 2))), ("space", "tm")
    )
    center = totals / count_all
    spread = squares / count_all - center * center
    return (center, lax.rsqrt(spread + EPSILON))


def normalize_act(values, stats, gain, shift):
    center, inverse = stats
    grouped = values.reshape(values.shape[:-1] + (NGROUP, values.shape[-1] // NGROUP))
    scaled = (grouped - center[:, None]) * inverse[:, None]
    return jax.nn.silu(scaled.reshape(values.shape) * gain + shift)


def tap_columns(padded, rows_out, cols_out):
    shifted = [
        padded[row_tap : row_tap + rows_out, col_tap : col_tap + cols_out, :]
        for row_tap in range(3)
        for col_tap in range(3)
    ]
    return jnp.stack(shifted, axis=2).reshape(rows_out * cols_out, 9, padded.shape[-1])


def add_taps(columns, piece):
    depth = piece.shape[2]
    picked = columns.reshape(columns.shape[0], 9 * depth)
    return jnp.dot(
        picked,
        piece.reshape(9 * depth, piece.shape[3]),
        precision=HIGHEST,
        preferred_element_type=jnp.float32,
    )


def wide_conv(padded, weight, rows_out, cols_out):
    columns = tap_columns(padded, rows_out, cols_out)
    summed = add_taps(columns, lax.all_gather(weight, "space", axis=2, tiled=True))
    return lax.all_gather(summed.reshape(rows_out, cols_out, -1), "chan", axis=2, tiled=True)


def border_rim(values):
    return padded_2(values, (("space", 0), ("tm", 1)), 1)


def on_device(
    features,
    norm1_gain,
    norm1_shift,
    conv1_weight,
    norm2_gain,
    norm2_shift,
    conv2_weight,
    head_gain,
    head_shift,
    head_weight,
    head_bias,
    noisy_latents,
    later_cond,
    patch_weight,
    patch_bias,
):
    tile_rows = features.shape[0]
    tile_cols = features.shape[1]
    count_all = float(
        tile_rows
        * tile_cols
        * lax.axis_size("space")
        * lax.axis_size("tm")
        * (features.shape[2] // NGROUP)
    )
    first_stats = group_stats(features, count_all)
    active = normalize_act(features, first_stats, norm1_gain, norm1_shift)
    first_conv = wide_conv(border_rim(active), conv1_weight, tile_rows, tile_cols)
    second_stats = group_stats(first_conv, count_all)
    second_act = normalize_act(first_conv, second_stats, norm2_gain, norm2_shift)
    second_conv = wide_conv(border_rim(second_act), conv2_weight, tile_rows, tile_cols)
    hidden = features + second_conv
    head_stats = group_stats(hidden, count_all)
    head_act = normalize_act(hidden, head_stats, head_gain, head_shift)
    head_pad = padded_2(head_act, (("space", 0), ("tm", 1)), 1)
    head_columns = tap_columns(head_pad, tile_rows, tile_cols)
    latent_part = (
        add_taps(head_columns, lax.all_gather(head_weight, "space", axis=2, tiled=True)) + head_bias
    )
    image_latent = lax.all_gather(
        latent_part.reshape(tile_rows, tile_cols, -1), "chan", axis=2, tiled=True
    )
    latent_row = lax.all_gather(image_latent, "tm", axis=1, tiled=True)
    frame_count = noisy_latents.shape[0]
    full_width = noisy_latents.shape[3]
    frame_ids = lax.axis_index("tm") * frame_count + jnp.arange(frame_count)
    opening = frame_ids == 0
    condition = jnp.where(
        opening[:, None, None, None], jnp.transpose(latent_row, (2, 0, 1))[None], later_cond
    )
    marks = jnp.broadcast_to(
        opening.astype(jnp.float32)[:, None, None, None], (frame_count, 4, tile_rows, full_width)
    )
    stacked = jnp.concatenate([noisy_latents, marks, condition], axis=1)
    channel_count = stacked.shape[1]
    patches = (
        stacked.reshape(frame_count, channel_count, tile_rows // 2, 2, full_width // 2, 2)
        .transpose(0, 2, 4, 1, 3, 5)
        .reshape(-1, channel_count * 4)
    )
    tokens = (
        jnp.dot(patches, patch_weight, precision=HIGHEST, preferred_element_type=jnp.float32)
        + patch_bias
    )
    return (tokens.reshape(frame_count, tile_rows // 2, full_width // 2, -1), image_latent)


def solution(mesh):
    return jax.shard_map(
        on_device,
        mesh=mesh,
        in_specs=(
            P(("groups", "space"), "tm", None),
            P(),
            P(),
            P(None, None, "space", "chan"),
            P(),
            P(),
            P(None, None, "space", "chan"),
            P(),
            P(),
            P(None, None, "space", "chan"),
            P("chan"),
            P(("groups", "tm"), None, "space", None),
            P(("groups", "tm"), None, "space", None),
            P(None, "chan"),
            P("chan"),
        ),
        out_specs=(P(("groups", "tm"), "space", None, "chan"), P(("groups", "space"), "tm", None)),
        check_vma=False,
    )
```

profile of v0, /device:TPU:0, one launch (start us, length us, event | category | flops | bytes accessed | tf_op | source)
XLA Modules:
  0.0 258.0 jit_solution(13659465206707186667)
XLA Ops:
  7.2 0.7 all-gather.3.cloned.1.call-update
  8.0 1.0 fusion.32
  9.2 0.1 reduce_sum.74
  9.3 0.1 reduce_sum.77
  9.4 23.8 %all-reduce.2 = (f32[32]{0:T(128)S(1)}, f32[32]{0:T(128)S(1)}) all-reduce(f32[32]{0:T(128)S(1)} %reduce_sum.77, f32[32]{0:T(128)S(1)} %reduce_sum.74), channel_id=1, replica_groups=mesh['groups'=2,'space'=4,'tm'=2,'chan'=2] {'space','tm'}, use_global_device_ids=true, to_apply=%region_5.6 | all-reduce | flops 64 | bytes 512 | tf_op jit(solution)/shard_map/psum | solution.py:32
  33.6 1.0 divide_multiply_fusion.2
  34.6 1.3 collective-permute-start
  35.9 1.3 collective-permute-start.1
  37.3 1.0 collective-permute-done
  38.3 6.3 %collective-permute-done.1 = f32[1,20,384]{2,1,0:T(8,128)S(1)} collective-permute-done((f32[1,20,384]{2,1,0:T(8,128)S(1)}, f32[1,20,384]{2,1,0:T(8,128)S(1)}, u32[]{:S(2)}, u32[]{:S(2)}) %collective-permute-start.1) | collective-permute-done | bytes 30752 | tf_op jit(solution)/shard_map/ppermute | solution.py:23
  44.7 1.3 collective-permute-start.2
  46.0 1.3 collective-permute-start.3
  47.4 4.2 %collective-permute-done.3 = f32[8,1,384]{2,0,1:T(8,128)S(1)} collective-permute-done((f32[8,1,384]{2,0,1:T(8,128)S(1)}, f32[8,1,384]{2,0,1:T(8,128)S(1)}, u32[]{:S(2)}, u32[]{:S(2)}) %collective-permute-start.3) | collective-permute-done | bytes 12320 | tf_op jit(solution)/shard_map/ppermute | solution.py:23
  52.0 0.6 copy-done.1
  52.9 2.3 copy.246
  55.2 2.0 dot_general.16
  57.2 25.8 %all-gather.3.cloned.1.call-done = f32[3,3,384,192]{3,2,1,0:T(8,128)} async-done(((f32[3,3,96,192]{3,2,1,0:T(8,128)}), f32[3,3,384,192]{3,2,1,0:T(8,128)}) %all-gather.3.cloned.1.call-update) | async-done | bytes 2654224 | tf_op jit(solution)/shard_map/all_gather | solution.py:69
  82.9 4.8 %fusion.42 = f32[6,20,192]{2,1,0:T(8,128)} fusion(f32[6,20,3456]{2,1,0:T(8,128)S(1)} %dot_general.16, f32[3456,192,1]{1,0,2:T(8,128)} %bitcast.136), kind=kOutput, calls=%fused_computation.100 | convolution fusion | flops 955514880 | bytes 4405248 | tf_op jit(solution)/shard_map/dot_general | solution.py:59
  87.7 2.1 copy.248
  89.8 3.1 %all_gather.22 = f32[6,20,384]{1,0,2:T(8,128)S(1)} all-gather(f32[6,20,192]{1,0,2:T(8,128)} %copy.248), channel_id=1, replica_groups=mesh['groups'=2,'space'=4,'tm'=2,'chan'=2] {'chan'}, dimensions={2}, use_global_device_ids=true | all-gather | bytes 276480 | tf_op jit(solution)/shard_map/all_gather | solution.py:70
  92.9 0.5 copy.249
  93.4 1.5 fusion.30
  95.0 0.1 reduce_sum.83
  95.2 0.1 reduce_sum.89
  95.3 20.1 %all-reduce.1 = (f32[32]{0:T(128)S(1)}, f32[32]{0:T(128)S(1)}) all-reduce(f32[32]{0:T(128)S(1)} %reduce_sum.89, f32[32]{0:T(128)S(1)} %reduce_sum.83), channel_id=1, replica_groups=mesh['groups'=2,'space'=4,'tm'=2,'chan'=2] {'space','tm'}, use_global_device_ids=true, to_apply=%region_11.12 | all-reduce | flops 64 | bytes 512 | tf_op jit(solution)/shard_map/psum | solution.py:32
  115.9 1.5 collective-permute-start.4
  117.4 1.3 collective-permute-start.5
  118.8 1.0 collective-permute-done.4
  119.9 6.6 %collective-permute-done.5 = f32[1,20,384]{2,1,0:T(8,128)S(1)} collective-permute-done((f32[1,20,384]{2,1,0:T(8,128)S(1)}, f32[1,20,384]{2,1,0:T(8,128)S(1)}, u32[]{:S(2)}, u32[]{:S(2)}) %collective-permute-start.5) | collective-permute-done | bytes 30752 | tf_op jit(solution)/shard_map/ppermute | solution.py:23
  126.5 1.3 collective-permute-start.6
  127.8 1.3 collective-permute-start.7
  129.2 4.2 %collective-permute-done.7 = f32[8,1,384]{2,0,1:T(8,128)S(1)} collective-permute-done((f32[8,1,384]{2,0,1:T(8,128)S(1)}, f32[8,1,384]{2,0,1:T(8,128)S(1)}, u32[]{:S(2)}, u32[]{:S(2)}) %collective-permute-start.7) | collective-permute-done | bytes 12320 | tf_op jit(solution)/shard_map/ppermute | solution.py:23
  134.0 2.2 copy.259
  136.2 2.0 dot_general.18
  138.2 15.9 %all-gather.5.cloned.1.call-done = f32[3,3,384,192]{3,2,1,0:T(8,128)} async-done(((f32[3,3,96,192]{3,2,1,0:T(8,128)}), f32[3,3,384,192]{3,2,1,0:T(8,128)}) %all-gather.5.cloned.1.call-update) | async-done | bytes 2654224 | tf_op jit(solution)/shard_map/all_gather | solution.py:69
  154.2 4.8 %fusion.43 = f32[6,20,192]{2,1,0:T(8,128)} fusion(f32[6,20,3456]{2,1,0:T(8,128)S(1)} %dot_general.18, f32[3456,192,1]{1,0,2:T(8,128)} %bitcast.135), kind=kOutput, calls=%fused_computation.101 | convolution fusion | flops 955514880 | bytes 4405248 | tf_op jit(solution)/shard_map/dot_general | solution.py:59
  158.9 2.1 copy.261
  161.0 3.4 %all_gather.24 = f32[6,20,384]{1,0,2:T(8,128)S(1)} all-gather(f32[6,20,192]{1,0,2:T(8,128)} %copy.261), channel_id=1, replica_groups=mesh['groups'=2,'space'=4,'tm'=2,'chan'=2] {'chan'}, dimensions={2}, use_global_device_ids=true | all-gather | bytes 276480 | tf_op jit(solution)/shard_map/all_gather | solution.py:70
  164.4 0.5 copy.262
  165.1 0.1 reduce_sum.110
  165.3 0.1 reduce_sum.113
  165.4 19.0 %all-reduce = (f32[32]{0:T(128)S(1)}, f32[32]{0:T(128)S(1)}) all-reduce(f32[32]{0:T(128)S(1)} %reduce_sum.113, f32[32]{0:T(128)S(1)} %reduce_sum.110), channel_id=1, replica_groups=mesh['groups'=2,'space'=4,'tm'=2,'chan'=2] {'space','tm'}, use_global_device_ids=true, to_apply=%region_17.18 | all-reduce | flops 64 | bytes 512 | tf_op jit(solution)/shard_map/psum | solution.py:32
  184.9 1.3 collective-permute-start.8
  186.2 1.3 collective-permute-start.9
  187.5 0.3 copy.273
  187.9 4.2 %collective-permute-done.9 = f32[1,20,384]{2,1,0:T(8,128)S(1)} collective-permute-done((f32[1,20,384]{2,1,0:T(8,128)S(1)}, f32[1,20,384]{2,1,0:T(8,128)S(1)}, u32[]{:S(2)}, u32[]{:S(2)}) %collective-permute-start.9) | collective-permute-done | bytes 30752 | tf_op jit(solution)/shard_map/ppermute | solution.py:23
  192.1 2.1 collective-permute-start.10
  194.2 1.4 collective-permute-start.11
  195.7 37.5 %all_gather.25 = f32[3,3,384,8]{3,1,0,2:T(4,128)} all-gather(f32[3,3,96,8]{3,1,0,2:T(4,128)S(1)} %copy.273), channel_id=1, replica_groups=mesh['groups'=2,'space'=4,'tm'=2,'chan'=2] {'space'}, dimensions={2}, use_global_device_ids=true | all-gather | bytes 138240 | tf_op jit(solution)/shard_map/all_gather | solution.py:115
  233.2 2.7 %copy.274 = f32[3,3,384,8]{2,3,1,0:T(8,128)S(1)} copy(f32[3,3,384,8]{3,1,0,2:T(4,128)} %all_gather.25) | data formatting | bytes 221184 | tf_op jit(solution)/shard_map/all_gather | solution.py:115
  235.9 0.1 copy.277
  236.0 0.1 copy.278
  236.8 0.7 copy.272
  237.5 0.5 copy.302
  238.2 1.5 convolution_add_fusion.1
  239.7 1.8 all_gather.26
  241.6 0.1 copy.276
  241.7 5.8 %all_gather.27 = f32[6,40,16]{2,0,1:T(8,128)S(1)} all-gather(f32[6,20,16]{2,0,1:T(8,128)S(1)} %copy.276), channel_id=1, replica_groups=mesh['groups'=2,'space'=4,'tm'=2,'chan'=2] {'tm'}, dimensions={1}, use_global_device_ids=true | all-gather | bytes 23040 | tf_op jit(solution)/shard_map/all_gather | solution.py:120
  247.5 0.1 pad_maximum_fusion.9
  247.7 0.3 copy.280
  247.9 0.2 reshape.82
  248.1 0.9 convolution_add_fusion
  249.0 1.6 reshape.86
  250.6 0.6 copy.382
  (115 shorter events, 4.5 us)
Async XLA Ops:
  7.2 240.9 %copy-start = (f32[144,2560]{1,0:T(8,128)S(1)}, f32[144,2560]{1,0:T(8,128)}, u32[]{:S(2)}) copy-start(f32[144,2560]{1,0:T(8,128)} %param.28) | copy-start | bytes 4423684
  7.2 75.8 %all-gather.3.cloned.1.call-start = ((), (), s32[]{:S(2)}) async-start(), calls=%async_computation | async-start | bytes 4423680 | tf_op jit(solution)/shard_map/all_gather | solution.py:69
  7.9 146.2 %all-gather.5.cloned.1.call-start = ((), (), s32[]{:S(2)}) async-start(), calls=%async_computation.1 | async-start | bytes 4423680 | tf_op jit(solution)/shard_map/all_gather | solution.py:69
  34.6 3.7 %collective-permute-start = (f32[1,20,384]{2,1,0:T(8,128)S(1)}, f32[1,20,384]{2,1,0:T(8,128)S(1)}, u32[]{:S(2)}, u32[]{:S(2)}) collective-permute-start(f32[1,20,384]{2,1,0:T(8,128)S(1)} %get-tuple-element.63), channel_id=1, source_target_pairs={{0,4},{4,8},{8,12},{1,5},{5,9},{9,13},{2,6},{6,10},{10,14},{3,7},{... | collective-permute-start | bytes 92168 | tf_op jit(solution)/shard_map/ppermute | solution.py:21
  35.9 8.7 %collective-permute-start.1 = (f32[1,20,384]{2,1,0:T(8,128)S(1)}, f32[1,20,384]{2,1,0:T(8,128)S(1)}, u32[]{:S(2)}, u32[]{:S(2)}) collective-permute-start(f32[1,20,384]{2,1,0:T(8,128)S(1)} %get-tuple-element.64), channel_id=1, source_target_pairs={{4,0},{8,4},{12,8},{5,1},{9,5},{13,9},{6,2},{10,6},{14,10},{7,3},{... | collective-permute-start | bytes 92168 | tf_op jit(solution)/shard_map/ppermute | solution.py:23
  44.7 2.7 %collective-permute-start.2 = (f32[8,1,384]{2,0,1:T(8,128)S(1)}, f32[8,1,384]{2,0,1:T(8,128)S(1)}, u32[]{:S(2)}, u32[]{:S(2)}) collective-permute-start(f32[8,1,384]{2,0,1:T(8,128)S(1)} %get-tuple-element.40), channel_id=1, source_target_pairs={{0,2},{1,3},{4,6},{5,7},{8,10},{9,11},{12,14},{13,15},{16,18},{17,... | collective-permute-start | bytes 36872 | tf_op jit(solution)/shard_map/ppermute | solution.py:21
  46.0 5.6 %collective-permute-start.3 = (f32[8,1,384]{2,0,1:T(8,128)S(1)}, f32[8,1,384]{2,0,1:T(8,128)S(1)}, u32[]{:S(2)}, u32[]{:S(2)}) collective-permute-start(f32[8,1,384]{2,0,1:T(8,128)S(1)} %get-tuple-element.39), channel_id=1, source_target_pairs={{2,0},{3,1},{6,4},{7,5},{10,8},{11,9},{14,12},{15,13},{18,16},{19,... | collective-permute-start | bytes 36872 | tf_op jit(solution)/shard_map/ppermute | solution.py:23
  51.7 0.9 copy-start.1
  51.7 0.9 copy-start.7
  51.7 0.9 copy-start.8
  92.9 22.9 %copy-start.9 = (f32[384]{0:T(512)S(1)}, f32[384]{0:T(512)}, u32[]{:S(2)}) copy-start(f32[384]{0:T(512)} %param.20) | copy-start | bytes 4612
  92.9 22.9 %copy-start.10 = (f32[384]{0:T(512)S(1)}, f32[384]{0:T(512)}, u32[]{:S(2)}) copy-start(f32[384]{0:T(512)} %param.19) | copy-start | bytes 4612
  115.9 3.9 %collective-permute-start.4 = (f32[1,20,384]{2,1,0:T(8,128)S(1)}, f32[1,20,384]{2,1,0:T(8,128)S(1)}, u32[]{:S(2)}, u32[]{:S(2)}) collective-permute-start(f32[1,20,384]{2,1,0:T(8,128)S(1)} %get-tuple-element.61), channel_id=1, source_target_pairs={{0,4},{4,8},{8,12},{1,5},{5,9},{9,13},{2,6},{6,10},{10,14},{3,7},{... | collective-permute-start | bytes 92168 | tf_op jit(solution)/shard_map/ppermute | solution.py:21
  117.4 9.0 %collective-permute-start.5 = (f32[1,20,384]{2,1,0:T(8,128)S(1)}, f32[1,20,384]{2,1,0:T(8,128)S(1)}, u32[]{:S(2)}, u32[]{:S(2)}) collective-permute-start(f32[1,20,384]{2,1,0:T(8,128)S(1)} %get-tuple-element.62), channel_id=1, source_target_pairs={{4,0},{8,4},{12,8},{5,1},{9,5},{13,9},{6,2},{10,6},{14,10},{7,3},{... | collective-permute-start | bytes 92168 | tf_op jit(solution)/shard_map/ppermute | solution.py:23
  126.5 2.7 %collective-permute-start.6 = (f32[8,1,384]{2,0,1:T(8,128)S(1)}, f32[8,1,384]{2,0,1:T(8,128)S(1)}, u32[]{:S(2)}, u32[]{:S(2)}) collective-permute-start(f32[8,1,384]{2,0,1:T(8,128)S(1)} %get-tuple-element.36), channel_id=1, source_target_pairs={{0,2},{1,3},{4,6},{5,7},{8,10},{9,11},{12,14},{13,15},{16,18},{17,... | collective-permute-start | bytes 36872 | tf_op jit(solution)/shard_map/ppermute | solution.py:21
  127.8 5.6 %collective-permute-start.7 = (f32[8,1,384]{2,0,1:T(8,128)S(1)}, f32[8,1,384]{2,0,1:T(8,128)S(1)}, u32[]{:S(2)}, u32[]{:S(2)}) collective-permute-start(f32[8,1,384]{2,0,1:T(8,128)S(1)} %get-tuple-element.35), channel_id=1, source_target_pairs={{2,0},{3,1},{6,4},{7,5},{10,8},{11,9},{14,12},{15,13},{18,16},{19,... | collective-permute-start | bytes 36872 | tf_op jit(solution)/shard_map/ppermute | solution.py:23
  161.0 3.9 %copy-start.2 = (f32[6,20,384]{2,1,0:T(8,128)S(1)}, f32[6,20,384]{2,1,0:T(8,128)}, u32[]{:S(2)}) copy-start(f32[6,20,384]{2,1,0:T(8,128)} %param.15) | copy-start | bytes 552964
  161.0 23.8 %copy-start.11 = (f32[384]{0:T(512)S(1)}, f32[384]{0:T(512)}, u32[]{:S(2)}) copy-start(f32[384]{0:T(512)} %param.23) | copy-start | bytes 4612
  161.0 23.8 %copy-start.12 = (f32[384]{0:T(512)S(1)}, f32[384]{0:T(512)}, u32[]{:S(2)}) copy-start(f32[384]{0:T(512)} %param.22) | copy-start | bytes 4612
  164.4 23.1 %copy-start.5 = (f32[3,3,96,8]{2,3,1,0:T(8,128)S(1)}, f32[3,3,96,8]{2,3,1,0:T(8,128)}, u32[]{:S(2)}) copy-start(f32[3,3,96,8]{2,3,1,0:T(8,128)} %param.24) | copy-start | bytes 82948
  184.9 2.9 %collective-permute-start.8 = (f32[1,20,384]{2,1,0:T(8,128)S(1)}, f32[1,20,384]{2,1,0:T(8,128)S(1)}, u32[]{:S(2)}, u32[]{:S(2)}) collective-permute-start(f32[1,20,384]{2,1,0:T(8,128)S(1)} %get-tuple-element.59), channel_id=1, source_target_pairs={{0,4},{4,8},{8,12},{1,5},{5,9},{9,13},{2,6},{6,10},{10,14},{3,7},{... | collective-permute-start | bytes 92168 | tf_op jit(solution)/shard_map/ppermute | solution.py:21
  186.2 5.9 %collective-permute-start.9 = (f32[1,20,384]{2,1,0:T(8,128)S(1)}, f32[1,20,384]{2,1,0:T(8,128)S(1)}, u32[]{:S(2)}, u32[]{:S(2)}) collective-permute-start(f32[1,20,384]{2,1,0:T(8,128)S(1)} %get-tuple-element.60), channel_id=1, source_target_pairs={{4,0},{8,4},{12,8},{5,1},{9,5},{13,9},{6,2},{10,6},{14,10},{7,3},{... | collective-permute-start | bytes 92168 | tf_op jit(solution)/shard_map/ppermute | solution.py:23
  192.1 44.1 %collective-permute-start.10 = (f32[8,1,384]{2,0,1:T(8,128)S(1)}, f32[8,1,384]{2,0,1:T(8,128)S(1)}, u32[]{:S(2)}, u32[]{:S(2)}) collective-permute-start(f32[8,1,384]{2,0,1:T(8,128)S(1)} %get-tuple-element.32), channel_id=1, source_target_pairs={{0,2},{1,3},{4,6},{5,7},{8,10},{9,11},{12,14},{13,15},{16,18},{17,... | collective-permute-start | bytes 36872 | tf_op jit(solution)/shard_map/ppermute | solution.py:21
  194.2 41.6 %copy-start.3 = (f32[1,16,6,40]{3,1,2,0:T(8,128)S(1)}, f32[1,16,6,40]{3,1,2,0:T(8,128)}, u32[]{:S(2)}) copy-start(f32[1,16,6,40]{3,1,2,0:T(8,128)} %param.27) | copy-start | bytes 46084
  194.2 42.0 %collective-permute-start.11 = (f32[8,1,384]{2,0,1:T(8,128)S(1)}, f32[8,1,384]{2,0,1:T(8,128)S(1)}, u32[]{:S(2)}, u32[]{:S(2)}) collective-permute-start(f32[8,1,384]{2,0,1:T(8,128)S(1)} %get-tuple-element.31), channel_id=1, source_target_pairs={{2,0},{3,1},{6,4},{7,5},{10,8},{11,9},{14,12},{15,13},{18,16},{19,... | collective-permute-start | bytes 36872 | tf_op jit(solution)/shard_map/ppermute | solution.py:23
  233.2 2.8 %copy-start.4 = (f32[1,16,6,40]{3,1,2,0:T(8,128)S(1)}, f32[1,16,6,40]{3,1,2,0:T(8,128)}, u32[]{:S(2)}) copy-start(f32[1,16,6,40]{3,1,2,0:T(8,128)} %param.26) | copy-start | bytes 46084
  237.5 0.7 copy-start.13
  238.2 10.0 %copy-start.6 = (f32[2560]{0:T(1024)S(1)}, f32[2560]{0:T(1024)}, u32[]{:S(2)}) copy-start(f32[2560]{0:T(1024)} %param.29) | copy-start | bytes 30724
Sparse Core Ops, SparseCore 0:
  9.6 73.3 all-gather.2
  84.5 69.5 all-gather.4
where the time goes:
time: 259 us; the launch traced here: 258 us
  blocking collectives  115 us (44%)
  waiting for transfers between devices  70.1 us (27%)
  local copies, waits for them, and re-layouts  24.7 us (10%)
  starting transfers between devices  16.8 us (6%)
  between operations  14.8 us (6%)
  matrix products  11.9 us (5%)
  other arithmetic  5.27 us (2%)
    psum x3, blocking collectives, group_stats(): lax.psum((jnp.sum(grouped, axis=(0, 2)), jnp.sum(grouped * grouped, axis=...  62.9 us
    all_gather x2, waiting for transfers between devices, wide_conv(): lax.all_gather(weight, 'space', axis=2, tiled=True)  41.7 us
    all_gather x1, blocking collectives, on_device(): lax.all_gather(head_weight, 'space', axis=2, tiled=True)  37.5 us
    ppermute x6, waiting for transfers between devices, padded_2(): lax.ppermute(head, axis, [((i + 1) % count, i) for i in range(ends)])  25.5 us
    dot_general x3, matrix products, add_taps(): jnp.dot(picked, piece.reshape(9 * depth, piece.shape[3]), precision=HIGHE...  11 us
    ppermute x6, starting transfers between devices, padded_2(): lax.ppermute(tail, axis, [(i, (i + 1) % count) for i in range(ends)])  8.79 us
    dot_general x4, local copies, waits for them, and re-layouts, add_taps(): jnp.dot(picked, piece.reshape(9 * depth, piece.shape[3]), precision=HIGHE...  8.15 us
    ppermute x6, starting transfers between devices, padded_2(): lax.ppermute(head, axis, [((i + 1) % count, i) for i in range(ends)])  7.88 us
  transfers between devices with their start and end apart: 14, of which 11 were waited for; matrix products, arithmetic and copies ran while one was open for 10% of the time, Pallas kernels for 0%

commit v1 on v0

--- a/solution.py
+++ b/solution.py
@@ -1,6 +1,10 @@
+import functools
+
 import jax
 import jax.numpy as jnp
 from jax import lax
+from jax.experimental import pallas as pl
+from jax.experimental.pallas import tpu as pltpu
 from jax.sharding import PartitionSpec as P
 
 NGROUP = 32
@@ -142,9 +146,620 @@
     return (tokens.reshape(frame_count, tile_rows // 2, full_width // 2, -1), image_latent)
 
 
+MESH = pl.DeviceIdType.MESH
+LANES = 128
+BF16 = jnp.bfloat16
+F32 = jnp.float32
+
+
+def split_pair(values):
+    high = values.astype(BF16)
+    return high, (values - high.astype(F32)).astype(BF16)
+
+
+def fused_kernel(
+    dims,
+    feat,
+    gain1,
+    shift1,
+    w1_hbm,
+    gain2,
+    shift2,
+    w2_hbm,
+    gain3,
+    shift3,
+    head_w,
+    head_b,
+    noisy,
+    later,
+    pw_hbm,
+    patch_b,
+    tokens,
+    latent,
+    w1_raw,
+    w2_raw,
+    pw_raw,
+    w1_mat,
+    w2_mat,
+    wh_mat,
+    wn_mat,
+    wc_mat,
+    base,
+    a_send,
+    feat_all,
+    conv_all,
+    taps,
+    msg,
+    msg_in,
+    piece,
+    piece_in,
+    lat_send,
+    lat_in,
+    cells,
+    turned,
+    patch,
+    load_sem,
+    a_ssem,
+    a_rsem,
+    m_ssem,
+    m_rsem,
+    sib_ssem,
+    sib_rsem,
+    p_ssem,
+    p_rsem,
+    l_ssem,
+    l_rsem,
+):
+    S, T, C = dims["S"], dims["T"], dims["C"]
+    R, W, CH = dims["R"], dims["W"], dims["CH"]
+    Z, FR = dims["Z"], dims["FR"]
+    CB = CH // S
+    NH = CH // C
+    BH = NH // CB
+    H = S * R
+    M = H * W
+    HM = M // 2
+    HR = H // 2
+    TILE = R * W
+    per_group = CH // NGROUP
+    ZH = Z // C
+    s = lax.axis_index("space")
+    t = lax.axis_index("tm")
+    c = lax.axis_index("chan")
+    other = 1 - c
+
+    loads = [
+        pltpu.make_async_copy(src, dst, load_sem.at[k])
+        for k, (src, dst) in enumerate(((w1_hbm, w1_raw), (w2_hbm, w2_raw)))
+    ]
+    strips = pw_raw.shape[0]
+    loads += [
+        pltpu.make_async_copy(
+            pw_hbm.at[:, n * LANES : (n + 1) * LANES], pw_raw.at[n], load_sem.at[2 + n]
+        )
+        for n in range(strips)
+    ]
+    for load in loads:
+        load.start()
+
+    barrier = pltpu.get_barrier_semaphore()
+    for ds in range(S):
+        for dt in range(T):
+            for dc in range(C):
+                if ds or dt or dc:
+                    pl.semaphore_signal(
+                        barrier,
+                        inc=1,
+                        device_id={
+                            "space": lax.rem(s + ds, S),
+                            "tm": lax.rem(t + dt, T),
+                            "chan": lax.rem(c + dc, C),
+                        },
+                        device_id_type=MESH,
+                    )
+
+    def padded(values, width):
+        rows = values.shape[0]
+        if width == values.shape[1]:
+            return values
+        return jnp.concatenate([values, jnp.zeros((rows, width - values.shape[1]), values.dtype)], axis=1)
+
+    for r in range(R):
+        line = feat[r]
+        for j in range(S):
+            a_send[j, r * W : (r + 1) * W, :] = padded(line[:, j * CB : (j + 1) * CB], LANES)
+
+    pl.semaphore_wait(barrier, S * T * C - 1)
+
+    def a_copy(step):
+        peer = lax.rem(s + step, S)
+        return pltpu.make_async_remote_copy(
+            src_ref=a_send.at[peer],
+            dst_ref=feat_all.at[pl.ds(pl.multiple_of(s * TILE, 8), TILE)],
+            send_sem=a_ssem.at[peer],
+            recv_sem=a_rsem.at[s],
+            device_id={"space": peer},
+            device_id_type=MESH,
+        )
+
+    def a_arrival(step):
+        peer = lax.rem(s + step, S)
+        return pltpu.make_async_remote_copy(
+            src_ref=a_send.at[peer],
+            dst_ref=feat_all.at[pl.ds(pl.multiple_of(peer * TILE, 8), TILE)],
+            send_sem=a_ssem.at[peer],
+            recv_sem=a_rsem.at[peer],
+            device_id={"space": peer},
+            device_id_type=MESH,
+        )
+
+    for step in range(1, S):
+        a_copy(step).start()
+    feat_all[pl.ds(pl.multiple_of(s * TILE, 8), TILE), :] = a_send[s]
+
+    def pick_block(ref):
+        row = ref[...]
+        out = jnp.zeros((1, CB), F32)
+        for j in range(S):
+            out = jnp.where(s == j, row[:, j * CB : (j + 1) * CB], out)
+        return padded(out, LANES)
+
+    row_id = lax.broadcasted_iota(jnp.int32, (LANES, LANES), 0)
+    col_id = lax.broadcasted_iota(jnp.int32, (LANES, LANES), 1)
+    same = ((row_id // per_group) == (col_id // per_group)) & (row_id < CB) & (col_id < CB)
+    member = jnp.where(same, 1.0, 0.0).astype(F32)
+
+    def group_sum(row):
+        wide = jnp.broadcast_to(row, (8, LANES))
+        return jnp.dot(wide, member, precision=HIGHEST, preferred_element_type=F32)[0:1]
+
+    def prepare(raw, mat):
+        gap = jnp.zeros((LANES - CB, BH * LANES), BF16) if CB < LANES else None
+        for tap in range(9):
+            w = raw[tap]
+            wide = jnp.concatenate(
+                [padded(w[:, i * CB : (i + 1) * CB], LANES) for i in range(BH)], axis=1
+            )
+            high, low = split_pair(wide)
+            store_split(mat, tap, high, low, gap)
+
+    def store_split(mat, tap, high, low, gap):
+        for place, value in ((2 * tap, high), (2 * tap + 1, high), (18 + tap, low)):
+            mat[place * LANES : place * LANES + CB, :] = value
+            if gap is not None:
+                mat[place * LANES + CB : (place + 1) * LANES, :] = gap
+
+    def channel_stats(values):
+        total = jnp.sum(values, axis=0, keepdims=True)
+        middle = total * (1.0 / HM)
+        away = values - middle
+        return total, jnp.sum(away * away, axis=0, keepdims=True)
+
+    edge = HR
+    pad_edge = dims["EDGE"]
+
+    def exchange(k, full):
+        start = pl.multiple_of(c * HM, 8)
+        total, spread = channel_stats(full[pl.ds(start, HM), :])
+        msg[k, 0:edge, :] = full[pl.ds(start, HR, stride=W), :]
+        msg[k, pad_edge : pad_edge + edge, :] = full[pl.ds(start + (W - 1), HR, stride=W), :]
+        msg[k, 2 * pad_edge : 2 * pad_edge + 1, :] = total
+        msg[k, 2 * pad_edge + 1 : 2 * pad_edge + 2, :] = spread
+
+        def copies(slot_t, slot_c, peer_t, peer_c, dc):
+            return pltpu.make_async_remote_copy(
+                src_ref=msg.at[k],
+                dst_ref=msg_in.at[k, slot_t, slot_c],
+                send_sem=m_ssem.at[k, peer_t, peer_c],
+                recv_sem=m_rsem.at[k, slot_t, slot_c],
+                device_id={"tm": peer_t, "chan": peer_c},
+                device_id_type=MESH,
+            )
+
+        outgoing = []
+        incoming = []
+        for dt in range(1, T):
+            for dc in range(C):
+                peer_t = lax.rem(t + dt, T)
+                peer_c = lax.rem(c + dc, C)
+                outgoing.append(copies(t, c, peer_t, peer_c, dc))
+                incoming.append(copies(peer_t, peer_c, peer_t, peer_c, dc))
+        for copy in outgoing:
+            copy.start()
+        return outgoing, incoming
+
+    def sibling(k, full, mine):
+        start = pl.multiple_of(mine * HM, 8)
+        return pltpu.make_async_remote_copy(
+            src_ref=full.at[pl.ds(start, HM)],
+            dst_ref=full.at[pl.ds(start, HM)],
+            send_sem=sib_ssem.at[k],
+            recv_sem=sib_rsem.at[k],
+            device_id={"chan": other},
+            device_id_type=MESH,
+        )
+
+    left = lax.rem(t + T - 1, T)
+    right = lax.rem(t + 1, T)
+
+    def activate(k, full, incoming, gain, shift):
+        parts = [channel_stats(full[h * HM : (h + 1) * HM, :]) for h in range(2)]
+        for copy in incoming:
+            copy.wait_recv()
+        for dt in range(1, T):
+            peer_t = lax.rem(t + dt, T)
+            for cc in range(C):
+                parts.append(
+                    (
+                        msg_in[k, peer_t, cc, 2 * pad_edge : 2 * pad_edge + 1, :],
+                        msg_in[k, peer_t, cc, 2 * pad_edge + 1 : 2 * pad_edge + 2, :],
+                    )
+                )
+        scale = 1.0 / float(per_group * M * T)
+        total = parts[0][0]
+        for part in parts[1:]:
+            total = total + part[0]
+        center = group_sum(total) * scale
+        gathered = jnp.zeros((1, LANES), F32)
+        for part_total, part_spread in parts:
+            away = part_total * (1.0 / HM) - center
+            gathered = gathered + part_spread + away * away * float(HM)
+        inverse = lax.rsqrt(group_sum(gathered) * scale + EPSILON)
+        multiply = inverse
+
+        def act(values):
+            u = (values - center) * multiply * gain + shift
+            return u / (1.0 + jnp.exp(-u))
+
+        for h in range(2):
+            value = act(full[h * HM : (h + 1) * HM, :])
+            at = W + h * HM
+            taps[1, at : at + HM, :] = value
+            taps[0, at + 1 : at + 1 + HM, :] = value
+            taps[2, at - 1 : at - 1 + HM, :] = value
+        for h in range(C):
+            from_left = act(msg_in[k, left, h, pad_edge : pad_edge + edge, :])
+            from_right = act(msg_in[k, right, h, 0:edge, :])
+            from_left = jnp.where(t > 0, from_left, 0.0)
+            from_right = jnp.where(t < T - 1, from_right, 0.0)
+            at = W + h * HM
+            taps[0, pl.ds(at, HR, stride=W), :] = from_left
+            taps[2, pl.ds(at + W - 1, HR, stride=W), :] = from_right
+        zero = jnp.zeros((W, LANES), F32)
+        tail = jnp.zeros((taps.shape[1] - W - M, LANES), F32)
+        for b in range(3):
+            taps[b, 0:W, :] = zero
+            taps[b, W + M :, :] = tail
+
+    def operand(start, rows):
+        pairs = []
+        for a in range(3):
+            for b in range(3):
+                pairs.append(split_pair(taps[b, start + a * W : start + a * W + rows, :]))
+        return jnp.concatenate(
+            [v for pair in pairs for v in pair] + [pair[0] for pair in pairs], axis=1
+        )
+
+    def piece_copy(k, i, h):
+        block = c * BH + i
+        return block, pltpu.make_async_remote_copy(
+            src_ref=piece.at[k, i, h],
+            dst_ref=piece_in.at[k, s],
+            send_sem=p_ssem.at[k, i, h],
+            recv_sem=p_rsem.at[k, s],
+            device_id={"space": block, "chan": h},
+            device_id_type=MESH,
+        )
+
+    def conv_send(k, mat):
+        for h in range(2):
+            part = jnp.dot(operand(h * HM, HM), mat[...], preferred_element_type=F32)
+            for i in range(BH):
+                piece[k, i, h] = part[:, i * LANES : (i + 1) * LANES]
+                block, copy = piece_copy(k, i, h)
+                away = jnp.logical_or(block != s, c != h)
+
+                @pl.when(away)
+                def _():
+                    copy.start()
+
+                @pl.when(jnp.logical_not(away))
+                def _():
+                    piece_in[k, s] = piece[k, i, h]
+
+    def conv_receive(k, full, extra):
+        holder = s // BH
+        for step in range(S):
+            source = lax.rem(s + step, S)
+            arrival = pltpu.make_async_remote_copy(
+                src_ref=piece.at[k, 0, 0],
+                dst_ref=piece_in.at[k, source],
+                send_sem=p_ssem.at[k, 0, 0],
+                recv_sem=p_rsem.at[k, source],
+                device_id={"space": source, "chan": holder},
+                device_id_type=MESH,
+            )
+            if step == 0:
+
+                @pl.when(holder != c)
+                def _():
+                    arrival.wait_recv()
+
+            else:
+                arrival.wait_recv()
+        total = piece_in[k, 0]
+        for j in range(1, S):
+            total = total + piece_in[k, j]
+        start = pl.multiple_of(c * HM, 8)
+        if extra is not None:
+            total = total + extra[pl.ds(start, HM), :]
+        full[pl.ds(start, HM), :] = total
+
+    def conv_drain(k):
+        for h in range(2):
+            for i in range(BH):
+                block, copy = piece_copy(k, i, h)
+
+                @pl.when(jnp.logical_or(block != s, c != h))
+                def _():
+                    copy.wait_send()
+
+    loads[0].wait()
+    prepare(w1_raw, w1_mat)
+    for step in range(1, S):
+        a_arrival(step).wait_recv()
+    out1, in1 = exchange(0, feat_all)
+    activate(0, feat_all, in1, pick_block(gain1), pick_block(shift1))
+    conv_send(0, w1_mat)
+
+    loads[1].wait()
+    prepare(w2_raw, w2_mat)
+    gap = jnp.zeros((LANES - CB, LANES), BF16) if CB < LANES else None
+    for tap in range(9):
+        high, low = split_pair(padded(head_w[tap], LANES))
+        store_split(wh_mat, tap, high, low, gap)
+    for load in loads[2:]:
+        load.wait()
+    for first, mat in ((0, wn_mat), (4 * (Z + 4), wc_mat)):
+        for b in range(2):
+            for a in range(2):
+                at = (b * 2 + a) * Z
+                for n in range(strips):
+                    high, low = split_pair(pw_raw[n, pl.ds(first + a * 2 + b, Z, stride=4), :])
+                    lanes = slice(n * LANES, (n + 1) * LANES)
+                    mat[at : at + Z, lanes] = high
+                    mat[4 * Z + at : 4 * Z + at + Z, lanes] = high
+                    mat[8 * Z + at : 8 * Z + at + Z, lanes] = low
+    mark_sum = jnp.concatenate(
+        [
+            jnp.sum(pw_raw[n, 4 * Z : 4 * (Z + 4), :], axis=0, keepdims=True)
+            for n in range(strips)
+        ],
+        axis=1,
+    )
+
+    PR, PC, PP = dims["PR"], dims["PC"], dims["PP"]
+    FULLW = W * T
+    cells[...] = jnp.zeros(cells.shape, F32)
+    patch[...] = jnp.zeros(patch.shape, F32)
+
+    def patches_of_cells():
+        turned[...] = cells[...].T
+        for b in range(2):
+            picked = turned[pl.ds(b, PC, stride=2), :]
+            for p in range(PR):
+                patch[p * PP : p * PP + PC, b * 2 * Z : (b + 1) * 2 * Z] = picked[
+                    :, p * 2 * Z : (p + 1) * 2 * Z
+                ]
+        high, low = split_pair(patch[:, 0 : 4 * Z])
+        return jnp.concatenate([high, low, high], axis=1)
+
+    for f in range(FR):
+        for i in range(R):
+            cells[i * Z : (i + 1) * Z, 0:FULLW] = noisy[f, :, i, :]
+        got = jnp.dot(patches_of_cells(), wn_mat[...], preferred_element_type=F32)
+        opening = (t * FR + f) == 0
+        base[f] = got + patch_b[...] + jnp.where(opening, mark_sum, 0.0)
+
+    conv_receive(0, conv_all.at[0], None)
+    sib1 = sibling(0, conv_all.at[0], c)
+    sib1.start()
+    out2, in2 = exchange(1, conv_all.at[0])
+    sibling(0, conv_all.at[0], other).wait_recv()
+    activate(1, conv_all.at[0], in2, pick_block(gain2), pick_block(shift2))
+    conv_send(1, w2_mat)
+
+    conv_receive(1, conv_all.at[1], feat_all)
+    sib2 = sibling(1, conv_all.at[1], c)
+    sib2.start()
+    out3, in3 = exchange(2, conv_all.at[1])
+    sibling(1, conv_all.at[1], other).wait_recv()
+    activate(2, conv_all.at[1], in3, pick_block(gain3), pick_block(shift3))
+
+    def lat_copy(dest_s, dest_t, dest_c, slot_s, slot_t, slot_c):
+        return pltpu.make_async_remote_copy(
+            src_ref=lat_send.at[dest_s],
+            dst_ref=lat_in.at[slot_t, slot_c, slot_s],
+            send_sem=l_ssem.at[dest_t, dest_c, dest_s],
+            recv_sem=l_rsem.at[slot_t, slot_c, slot_s],
+            device_id={"space": dest_s, "tm": dest_t, "chan": dest_c},
+            device_id_type=MESH,
+        )
+
+    bias = jnp.where(s == 0, head_b[...], 0.0)
+    for j in range(S):
+        part = jnp.dot(operand(j * TILE, LANES), wh_mat[...], preferred_element_type=F32)
+        lat_send[j] = part.T[0:ZH, :] + bias
+    lat_in[t, c, s] = lat_send[s]
+    lat_out = []
+    lat_arrive = []
+    for ds in reversed(range(S)):
+        for dt in range(T):
+            for dc in range(C):
+                if ds or dt or dc:
+                    ps = lax.rem(s + ds, S)
+                    pt = lax.rem(t + dt, T)
+                    pc = lax.rem(c + dc, C)
+                    copy = lat_copy(ps, pt, pc, s, t, c)
+                    copy.start()
+                    lat_out.append(copy)
+                    lat_arrive.append(lat_copy(ps, pt, pc, ps, pt, pc))
+
+    conv_drain(0)
+    conv_drain(1)
+    for copy in out1 + out2 + out3 + [sib1, sib2]:
+        copy.wait_send()
+    for step in range(1, S):
+        a_copy(step).wait_send()
+
+    for copy in lat_arrive:
+        copy.wait_recv()
+
+    def half_latent(tt, cc):
+        total = lat_in[tt, cc, 0]
+        for j in range(1, S):
+            total = total + lat_in[tt, cc, j]
+        return total
+
+    cells[...] = jnp.zeros(cells.shape, F32)
+    for cc in range(C):
+        cells[cc * ZH : (cc + 1) * ZH, :] = half_latent(t, cc)
+    turned[...] = cells[...].T
+    for r in range(R):
+        latent[r] = turned[r * W : (r + 1) * W, 0:Z]
+    for f in range(FR):
+        cells[...] = jnp.zeros(cells.shape, F32)
+        opening = (t * FR + f) == 0
+        for tt in range(T):
+            for cc in range(C):
+                value = half_latent(tt, cc)
+                for i in range(R):
+                    at = i * Z + cc * ZH
+                    cells[at : at + ZH, tt * W : (tt + 1) * W] = value[:, i * W : (i + 1) * W]
+        for i in range(R):
+            rows = slice(i * Z, (i + 1) * Z)
+            cells[rows, 0:FULLW] = jnp.where(opening, cells[rows, 0:FULLW], later[f, :, i, :])
+        got = base[f] + jnp.dot(patches_of_cells(), wc_mat[...], preferred_element_type=F32)
+        for p in range(PR):
+            tokens[f, p] = got[p * PP : p * PP + PC, :]
+    for copy in lat_out:
+        copy.wait_send()
+
+
+def up(value, unit):
+    return -(-value // unit) * unit
+
+
+def plan(mesh_shape, features, noisy_latents, patch_weight):
+    S, T, C = mesh_shape["space"], mesh_shape["tm"], mesh_shape["chan"]
+    R, W, CH = features.shape
+    FR, Z = noisy_latents.shape[:2]
+    dims = dict(S=S, T=T, C=C, R=R, W=W, CH=CH, Z=Z, FR=FR)
+    H = S * R
+    dims["EDGE"] = up(H // 2, 8)
+    dims["PR"], dims["PC"] = R // 2, W * T // 2
+    dims["PP"] = up(W * T // 2, 8)
+    dims["N"] = patch_weight.shape[1]
+    fits = (
+        C == 2
+        and T > 1
+        and S % C == 0
+        and CH % S == 0
+        and CH // S <= LANES
+        and (CH // S) % (CH // NGROUP) == 0
+        and (R * W) % 8 == 0
+        and (H * W // 2) % 8 == 0
+        and H % 2 == 0
+        and R * W <= LANES
+        and R * Z <= LANES
+        and W * T <= LANES
+        and 4 * Z <= LANES
+        and dims["N"] % LANES == 0
+        and H * W * LANES * 4 <= 2**19
+    )
+    return dims if fits else None
+
+
+def fused(dims, args):
+    S, T, C = dims["S"], dims["T"], dims["C"]
+    R, W, CH = dims["R"], dims["W"], dims["CH"]
+    Z, FR, N, EDGE = dims["Z"], dims["FR"], dims["N"], dims["EDGE"]
+    CB, NH = CH // S, CH // C
+    BH = NH // CB
+    M = S * R * W
+    MR = 2 * EDGE + 8
+    (f, g1, s1, w1, g2, s2, w2, g3, s3, hw, hb, noisy, later, pw, pb) = args
+    row = lambda v: v.reshape(1, v.shape[0])
+    flat = lambda v: v.reshape((9,) + v.shape[2:])
+    operands = (
+        f, row(g1), row(s1), flat(w1), row(g2), row(s2), flat(w2), row(g3), row(s3),
+        flat(hw), hb.reshape(-1, 1), noisy, later, pw, row(pb),
+    )
+    vmem = pl.BlockSpec(memory_space=pltpu.VMEM)
+    far = pl.BlockSpec(memory_space=pl.ANY)
+    in_specs = [far if k in (3, 6, 13) else vmem for k in range(15)]
+    dma = pltpu.SemaphoreType.DMA
+    big = lambda n: pltpu.VMEM((27 * LANES, n), BF16)
+    scratch = [
+        pltpu.VMEM((9, CB, NH), F32),
+        pltpu.VMEM((9, CB, NH), F32),
+        pltpu.VMEM((N // LANES, pw.shape[0], LANES), F32),
+        big(BH * LANES),
+        big(BH * LANES),
+        big(LANES),
+        pltpu.VMEM((12 * Z, N), BF16),
+        pltpu.VMEM((12 * Z, N), BF16),
+        pltpu.VMEM((FR, dims["PR"] * dims["PP"], N), F32),
+        pltpu.VMEM((S, R * W, LANES), F32),
+        pltpu.VMEM((M, LANES), F32),
+        pltpu.VMEM((2, M, LANES), F32),
+        pltpu.VMEM((3, up(M + 2 * W + LANES, 8), LANES), F32),
+        pltpu.VMEM((3, MR, LANES), F32),
+        pltpu.VMEM((3, T, C, MR, LANES), F32),
+        pltpu.VMEM((2, BH, 2, M // 2, LANES), F32),
+        pltpu.VMEM((2, S, M // 2, LANES), F32),
+        pltpu.VMEM((S, Z // C, LANES), F32),
+        pltpu.VMEM((T, C, S, Z // C, LANES), F32),
+        pltpu.VMEM((LANES, LANES), F32),
+        pltpu.VMEM((LANES, LANES), F32),
+        pltpu.VMEM((dims["PR"] * dims["PP"], LANES), F32),
+        dma((2 + N // LANES,)),
+        dma((S,)),
+        dma((S,)),
+        dma((3, T, C)),
+        dma((3, T, C)),
+        dma((2,)),
+        dma((2,)),
+        dma((2, BH, 2)),
+        dma((2, S)),
+        dma((T, C, S)),
+        dma((T, C, S)),
+    ]
+    return pl.pallas_call(
+        functools.partial(fused_kernel, dims),
+        out_shape=(
+            jax.ShapeDtypeStruct((FR, dims["PR"], dims["PC"], N), F32),
+            jax.ShapeDtypeStruct((R, W, Z), F32),
+        ),
+        in_specs=in_specs,
+        out_specs=(vmem, vmem),
+        scratch_shapes=scratch,
+        compiler_params=pltpu.CompilerParams(
+            collective_id=0, has_side_effects=True, vmem_limit_bytes=60 * 2**20
+        ),
+        name="fused_block",
+    )(*operands)
+
+
 def solution(mesh):
+    shape = dict(mesh.shape)
+
+    def step(*args):
+        dims = plan(shape, args[0], args[11], args[13])
+        return on_device(*args) if dims is None else fused(dims, args)
+
     return jax.shard_map(
-        on_device,
+        step,
         mesh=mesh,
         in_specs=(
             P(("groups", "space"), "tm", None),

time: 259 us -> 76 us (0.29)
  blocking collectives: 115 us -> 0 us
  waiting for transfers between devices: 70.1 us -> 0 us
  Pallas kernels: 0 us -> 55.7 us
  starting transfers between devices: 16.8 us -> 0 us
  between operations: 14.8 us -> 0.64 us
  matrix products: 11.9 us -> 0 us
  local copies, waits for them, and re-layouts: 24.7 us -> 19 us
  other arithmetic: 5.27 us -> 0 us
    psum x3 -> x0, blocking collectives: 62.9 us -> none  [group_stats(): lax.psum((jnp.sum(grouped, axis=(0, 2)), jnp.sum(grouped * grouped, axis=...]
    pallas_call x0 -> x1, Pallas kernels: none -> 55.7 us  [fused(): pl.pallas_call(functools.partial(fused_kernel, dims), out_shape=(jax.Shap...]
    all_gather x5 -> x0, blocking collectives: 51.7 us -> none  [the longest x1 37.5 us: on_device(): lax.all_gather(head_weight, 'space', axis=2, tiled=True)]
    all_gather x2 -> x0, waiting for transfers between devices: 41.7 us -> none  [wide_conv(): lax.all_gather(weight, 'space', axis=2, tiled=True)]
    ppermute x12 -> x0, waiting for transfers between devices: 27.7 us -> none  [the longest x6 25.5 us: padded_2(): lax.ppermute(head, axis, [((i + 1) % count, i) for i in range(ends)])]
    ppermute x12 -> x0, starting transfers between devices: 16.7 us -> none  [the longest x6 8.79 us: padded_2(): lax.ppermute(tail, axis, [(i, (i + 1) % count) for i in range(ends)])]
    dot_general x4 -> x0, matrix products: 11.9 us -> none  [the longest x3 11 us: add_taps(): jnp.dot(picked, piece.reshape(9 * depth, piece.shape[3]), precision=HIGHE...]
    reshape x4 -> x8, local copies, waits for them, and re-layouts: 1.79 us -> 10.2 us  [the longest x7 8.92 us: fused(): row = lambda v: v.reshape(1, v.shape[0])]
  transfers between devices with their start and end apart: 14 -> 0, of which waited for: 11 -> 0; matrix products, arithmetic and copies ran while one was open for 10% -> 0% of each run, Pallas kernels for 0% -> 0%
where the time goes in v1:
time: 76 us; the launch traced here: 75.4 us
  Pallas kernels  55.7 us (73%)
  local copies, waits for them, and re-layouts  19 us (25%)
    pallas_call x1, Pallas kernels, fused(): pl.pallas_call(functools.partial(fused_kernel, dims), out_shape=(jax.Shap...  55.7 us
    reshape x7, local copies, waits for them, and re-layouts, fused(): row = lambda v: v.reshape(1, v.shape[0])  8.92 us
    unnamed x3, local copies, waits for them, and re-layouts  4.61 us
    pallas_call x2, local copies, waits for them, and re-layouts, fused(): pl.pallas_call(functools.partial(fused_kernel, dims), out_shape=(jax.Shap...  4.18 us

profile of v1, /device:TPU:0, one launch (start us, length us, event | category | flops | bytes accessed | tf_op | source)
XLA Modules:
  0.0 75.4 jit_solution(15655507312549538422)
XLA Ops:
  0.6 1.3 %reshape.37.gain1 = f32[1,384]{1,0:T(1,128)} reshape(f32[384]{0:T(512)} %param.16) | data formatting | bytes 3072 | tf_op jit(solution)/shard_map/reshape | solution.py:692
  1.9 1.3 %reshape.38.shift1 = f32[1,384]{1,0:T(1,128)} reshape(f32[384]{0:T(512)} %param.17) | data formatting | bytes 3072 | tf_op jit(solution)/shard_map/reshape | solution.py:692
  3.2 1.3 %reshape.40.gain2 = f32[1,384]{1,0:T(1,128)} reshape(f32[384]{0:T(512)} %param.19) | data formatting | bytes 3072 | tf_op jit(solution)/shard_map/reshape | solution.py:692
  4.4 1.3 %reshape.41.shift2 = f32[1,384]{1,0:T(1,128)} reshape(f32[384]{0:T(512)} %param.20) | data formatting | bytes 3072 | tf_op jit(solution)/shard_map/reshape | solution.py:692
  5.7 1.3 %reshape.43.gain3 = f32[1,384]{1,0:T(1,128)} reshape(f32[384]{0:T(512)} %param.22) | data formatting | bytes 3072 | tf_op jit(solution)/shard_map/reshape | solution.py:692
  7.0 1.3 %reshape.44.shift3 = f32[1,384]{1,0:T(1,128)} reshape(f32[384]{0:T(512)} %param.23) | data formatting | bytes 3072 | tf_op jit(solution)/shard_map/reshape | solution.py:692
  8.2 1.3 %copy.18.head_b = f32[8,1]{1,0:T(8,128)} copy(f32[8,1]{0,1:T(1,128)} %bitcast.7) | data formatting | bytes 64 | tf_op jit(solution)/shard_map/reshape | solution.py:696
  9.6 1.3 %reshape.47.patch_b = f32[1,2560]{1,0:T(1,128)} reshape(f32[2560]{0:T(1024)} %param.29) | data formatting | bytes 20480 | tf_op jit(solution)/shard_map/reshape | solution.py:692
  10.9 1.4 %copy.19.noisy = f32[1,16,6,40]{3,2,1,0:T(8,128)} copy(f32[1,16,6,40]{3,1,2,0:T(8,128)} %param.26) | data formatting | bytes 30720 | tf_op args[11]
  12.3 1.4 %copy.20.later = f32[1,16,6,40]{3,2,1,0:T(8,128)} copy(f32[1,16,6,40]{3,1,2,0:T(8,128)} %param.27) | data formatting | bytes 30720 | tf_op args[12]
  13.7 1.7 %copy.17 = f32[3,3,96,8]{3,2,1,0:T(8,128)} copy(f32[3,3,96,8]{2,3,1,0:T(8,128)} %param.24) | data formatting | bytes 55296 | tf_op args[9]
  15.5 55.7 %fused_block.1 = (f32[1,3,20,2560]{3,2,1,0:T(8,128)}, f32[6,20,16]{2,1,0:T(8,128)}) custom-call(f32[6,20,384]{2,1,0:T(8,128)} %feat.1, f32[1,384]{1,0:T(1,128)} %reshape.37.gain1, f32[1,384]{1,0:T(1,128)} %reshape.38.shift1, f32[9,96,192]{2,1,0:T(8,128)} %bitcast.5, f32[1,384]{1,0:T(1,128)} %reshape.40.gain2, f32[1,384]{1,0:T(1,128)} %reshape.41.shift2, ...), custom_call_target="tpu_custom_call" | custom-call | tf_op jit(solution)/shard_map/fused_block/pallas_call | solution.py:738
  71.2 2.6 %copy.21 = f32[1,3,20,2560]{3,0,2,1:T(1,128)} copy(f32[1,3,20,2560]{3,2,1,0:T(8,128)} %get-tuple-element.2) | data formatting | bytes 1228800 | tf_op jit(solution)/shard_map/fused_block/pallas_call | solution.py:738
  73.8 1.6 %copy.22 = f32[6,20,16]{1,2,0:T(8,128)} copy(f32[6,20,16]{2,1,0:T(8,128)} %get-tuple-element.3) | data formatting | bytes 15360 | tf_op jit(solution)/shard_map/fused_block/pallas_call | solution.py:738

commit v2 on v1

--- a/solution.py
+++ b/solution.py
@@ -159,23 +159,35 @@
 
 def fused_kernel(
     dims,
+    feat_hbm,
+    gain1_hbm,
+    shift1_hbm,
+    w1_hbm,
+    gain2_hbm,
+    shift2_hbm,
+    w2_hbm,
+    gain3_hbm,
+    shift3_hbm,
+    head_w_hbm,
+    head_b_hbm,
+    noisy_hbm,
+    later_hbm,
+    pw_hbm,
+    patch_b_hbm,
+    tokens,
+    latent,
     feat,
     gain1,
     shift1,
-    w1_hbm,
     gain2,
     shift2,
-    w2_hbm,
     gain3,
     shift3,
     head_w,
     head_b,
     noisy,
     later,
-    pw_hbm,
     patch_b,
-    tokens,
-    latent,
     w1_raw,
     w2_raw,
     pw_raw,
@@ -228,14 +240,19 @@
     c = lax.axis_index("chan")
     other = 1 - c
 
+    early = (
+        (feat_hbm, feat), (w1_hbm, w1_raw), (gain1_hbm, gain1), (shift1_hbm, shift1),
+        (w2_hbm, w2_raw), (gain2_hbm, gain2), (shift2_hbm, shift2),
+        (gain3_hbm, gain3), (shift3_hbm, shift3), (head_w_hbm, head_w), (head_b_hbm, head_b),
+        (noisy_hbm, noisy), (later_hbm, later), (patch_b_hbm, patch_b),
+    )
     loads = [
-        pltpu.make_async_copy(src, dst, load_sem.at[k])
-        for k, (src, dst) in enumerate(((w1_hbm, w1_raw), (w2_hbm, w2_raw)))
+        pltpu.make_async_copy(src, dst, load_sem.at[k]) for k, (src, dst) in enumerate(early)
     ]
     strips = pw_raw.shape[0]
     loads += [
         pltpu.make_async_copy(
-            pw_hbm.at[:, n * LANES : (n + 1) * LANES], pw_raw.at[n], load_sem.at[2 + n]
+            pw_hbm.at[:, n * LANES : (n + 1) * LANES], pw_raw.at[n], load_sem.at[len(early) + n]
         )
         for n in range(strips)
     ]
@@ -264,6 +281,7 @@
             return values
         return jnp.concatenate([values, jnp.zeros((rows, width - values.shape[1]), values.dtype)], axis=1)
 
+    loads[0].wait()
     for r in range(R):
         line = feat[r]
         for j in range(S):
@@ -298,7 +316,7 @@
     feat_all[pl.ds(pl.multiple_of(s * TILE, 8), TILE), :] = a_send[s]
 
     def pick_block(ref):
-        row = ref[...]
+        row = ref[...].reshape(1, CH)
         out = jnp.zeros((1, CB), F32)
         for j in range(S):
             out = jnp.where(s == j, row[:, j * CB : (j + 1) * CB], out)
@@ -504,7 +522,8 @@
                 def _():
                     copy.wait_send()
 
-    loads[0].wait()
+    for load in loads[1:4]:
+        load.wait()
     prepare(w1_raw, w1_mat)
     for step in range(1, S):
         a_arrival(step).wait_recv()
@@ -512,14 +531,13 @@
     activate(0, feat_all, in1, pick_block(gain1), pick_block(shift1))
     conv_send(0, w1_mat)
 
-    loads[1].wait()
+    for load in loads[4:]:
+        load.wait()
     prepare(w2_raw, w2_mat)
-    gap = jnp.zeros((LANES - CB, LANES), BF16) if CB < LANES else None
     for tap in range(9):
         high, low = split_pair(padded(head_w[tap], LANES))
-        store_split(wh_mat, tap, high, low, gap)
-    for load in loads[2:]:
-        load.wait()
+        for place, value in ((2 * tap, high), (2 * tap + 1, high), (18 + tap, low)):
+            wh_mat[:, place * LANES : (place + 1) * LANES] = value
     for first, mat in ((0, wn_mat), (4 * (Z + 4), wc_mat)):
         for b in range(2):
             for a in range(2):
@@ -556,10 +574,10 @@
 
     for f in range(FR):
         for i in range(R):
-            cells[i * Z : (i + 1) * Z, 0:FULLW] = noisy[f, :, i, :]
+            cells[i * Z : (i + 1) * Z, 0:FULLW] = noisy[f, i]
         got = jnp.dot(patches_of_cells(), wn_mat[...], preferred_element_type=F32)
         opening = (t * FR + f) == 0
-        base[f] = got + patch_b[...] + jnp.where(opening, mark_sum, 0.0)
+        base[f] = got + patch_b[...].reshape(1, -1) + jnp.where(opening, mark_sum, 0.0)
 
     conv_receive(0, conv_all.at[0], None)
     sib1 = sibling(0, conv_all.at[0], c)
@@ -586,10 +604,19 @@
             device_id_type=MESH,
         )
 
-    bias = jnp.where(s == 0, head_b[...], 0.0)
+    bias_row = jnp.broadcast_to(head_b[...].reshape(1, ZH), (ZH, ZH))
+    diagonal = lax.broadcasted_iota(jnp.int32, (ZH, ZH), 0) == lax.broadcasted_iota(
+        jnp.int32, (ZH, ZH), 1
+    )
+    bias = jnp.sum(jnp.where(diagonal & (s == 0), bias_row, 0.0), axis=1, keepdims=True)
     for j in range(S):
-        part = jnp.dot(operand(j * TILE, LANES), wh_mat[...], preferred_element_type=F32)
-        lat_send[j] = part.T[0:ZH, :] + bias
+        part = lax.dot_general(
+            wh_mat[...],
+            operand(j * TILE, LANES),
+            (((1,), (1,)), ((), ())),
+            preferred_element_type=F32,
+        )
+        lat_send[j] = part + bias
     lat_in[t, c, s] = lat_send[s]
     lat_out = []
     lat_arrive = []
@@ -621,12 +648,10 @@
             total = total + lat_in[tt, cc, j]
         return total
 
-    cells[...] = jnp.zeros(cells.shape, F32)
     for cc in range(C):
-        cells[cc * ZH : (cc + 1) * ZH, :] = half_latent(t, cc)
-    turned[...] = cells[...].T
-    for r in range(R):
-        latent[r] = turned[r * W : (r + 1) * W, 0:Z]
+        value = half_latent(t, cc)
+        for r in range(R):
+            latent[r, cc * ZH : (cc + 1) * ZH, :] = value[:, r * W : (r + 1) * W]
     for f in range(FR):
         cells[...] = jnp.zeros(cells.shape, F32)
         opening = (t * FR + f) == 0
@@ -638,10 +663,10 @@
                     cells[at : at + ZH, tt * W : (tt + 1) * W] = value[:, i * W : (i + 1) * W]
         for i in range(R):
             rows = slice(i * Z, (i + 1) * Z)
-            cells[rows, 0:FULLW] = jnp.where(opening, cells[rows, 0:FULLW], later[f, :, i, :])
+            cells[rows, 0:FULLW] = jnp.where(opening, cells[rows, 0:FULLW], later[f, i])
         got = base[f] + jnp.dot(patches_of_cells(), wc_mat[...], preferred_element_type=F32)
         for p in range(PR):
-            tokens[f, p] = got[p * PP : p * PP + PC, :]
+            tokens[p, :, f, :] = got[p * PP : p * PP + PC, :]
     for copy in lat_out:
         copy.wait_send()
 
@@ -689,24 +714,25 @@
     M = S * R * W
     MR = 2 * EDGE + 8
     (f, g1, s1, w1, g2, s2, w2, g3, s3, hw, hb, noisy, later, pw, pb) = args
-    row = lambda v: v.reshape(1, v.shape[0])
     flat = lambda v: v.reshape((9,) + v.shape[2:])
+    by_row = lambda v: jnp.transpose(v, (0, 2, 1, 3))
     operands = (
-        f, row(g1), row(s1), flat(w1), row(g2), row(s2), flat(w2), row(g3), row(s3),
-        flat(hw), hb.reshape(-1, 1), noisy, later, pw, row(pb),
+        f, g1, s1, flat(w1), g2, s2, flat(w2), g3, s3,
+        flat(jnp.transpose(hw, (0, 1, 3, 2))), hb, by_row(noisy), by_row(later), pw, pb,
     )
     vmem = pl.BlockSpec(memory_space=pltpu.VMEM)
-    far = pl.BlockSpec(memory_space=pl.ANY)
-    in_specs = [far if k in (3, 6, 13) else vmem for k in range(15)]
+    in_specs = [pl.BlockSpec(memory_space=pl.ANY)] * 15
     dma = pltpu.SemaphoreType.DMA
     big = lambda n: pltpu.VMEM((27 * LANES, n), BF16)
     scratch = [
+        pltpu.VMEM(operands[k].shape, F32) for k in (0, 1, 2, 4, 5, 7, 8, 9, 10, 11, 12, 14)
+    ] + [
         pltpu.VMEM((9, CB, NH), F32),
         pltpu.VMEM((9, CB, NH), F32),
         pltpu.VMEM((N // LANES, pw.shape[0], LANES), F32),
         big(BH * LANES),
         big(BH * LANES),
-        big(LANES),
+        pltpu.VMEM((Z // C, 27 * LANES), BF16),
         pltpu.VMEM((12 * Z, N), BF16),
         pltpu.VMEM((12 * Z, N), BF16),
         pltpu.VMEM((FR, dims["PR"] * dims["PP"], N), F32),
@@ -723,7 +749,7 @@
         pltpu.VMEM((LANES, LANES), F32),
         pltpu.VMEM((LANES, LANES), F32),
         pltpu.VMEM((dims["PR"] * dims["PP"], LANES), F32),
-        dma((2 + N // LANES,)),
+        dma((14 + N // LANES,)),
         dma((S,)),
         dma((S,)),
         dma((3, T, C)),
@@ -735,11 +761,11 @@
         dma((T, C, S)),
         dma((T, C, S)),
     ]
-    return pl.pallas_call(
+    tokens, latent = pl.pallas_call(
         functools.partial(fused_kernel, dims),
         out_shape=(
-            jax.ShapeDtypeStruct((FR, dims["PR"], dims["PC"], N), F32),
-            jax.ShapeDtypeStruct((R, W, Z), F32),
+            jax.ShapeDtypeStruct((dims["PR"], dims["PC"], FR, N), F32),
+            jax.ShapeDtypeStruct((R, Z, W), F32),
         ),
         in_specs=in_specs,
         out_specs=(vmem, vmem),
@@ -749,6 +775,7 @@
         ),
         name="fused_block",
     )(*operands)
+    return jnp.transpose(tokens, (2, 0, 1, 3)), jnp.transpose(latent, (0, 2, 1))
 
 
 def solution(mesh):

time: 76 us -> 58.9 us (0.78)
  local copies, waits for them, and re-layouts: 19 us -> 3.37 us
  Pallas kernels: 55.7 us -> 54.7 us
    reshape x8 -> x0, local copies, waits for them, and re-layouts: 10.2 us -> none  [the longest x7 8.92 us: fused(): row = lambda v: v.reshape(1, v.shape[0])]
    pallas_call x2 -> x0, local copies, waits for them, and re-layouts: 4.18 us -> none  [fused(): pl.pallas_call(functools.partial(fused_kernel, dims), out_shape=(jax.Shap...]
    unnamed x3 -> x2, local copies, waits for them, and re-layouts: 4.61 us -> 3.37 us
    pallas_call x1, Pallas kernels: 55.7 us -> 54.7 us  [fused(): pl.pallas_call(functools.partial(fused_kernel, dims), out_shape=(jax.Shap...]
where the time goes in v2:
time: 58.9 us; the launch traced here: 58.7 us
  Pallas kernels  54.7 us (93%)
  local copies, waits for them, and re-layouts  3.37 us (6%)
  between operations  0.64 us (1%)
    pallas_call x1, Pallas kernels, fused(): pl.pallas_call(functools.partial(fused_kernel, dims), out_shape=(jax.Shap...  54.7 us
    unnamed x2, local copies, waits for them, and re-layouts  3.37 us

profile of v2, /device:TPU:0, one launch (start us, length us, event | category | flops | bytes accessed | tf_op | source)
XLA Modules:
  0.0 58.7 jit_solution(17450010197169802453)
XLA Ops:
  0.6 54.7 %fused_block.1 = (f32[3,20,1,2560]{3,2,1,0:T(1,128)}, f32[6,16,20]{2,1,0:T(8,128)}) custom-call(f32[6,20,384]{2,1,0:T(8,128)} %feat_hbm.1, f32[384]{0:T(512)} %gain1_hbm.1, f32[384]{0:T(512)} %shift1_hbm.1, f32[9,96,192]{2,1,0:T(8,128)} %bitcast.9, f32[384]{0:T(512)} %gain2_hbm.1, f32[384]{0:T(512)} %shift2_hbm.1, f32[9,96,192]{2,1,0:T(8,128)} %bitcast.10, ...), custom_call_target="tpu_custom_call" | custom-call | tf_op jit(solution)/shard_map/fused_block/pallas_call | solution.py:764
  55.4 1.9 %copy.19 = f32[1,3,20,2560]{3,0,2,1:T(1,128)} copy(f32[1,3,20,2560]{3,0,2,1:T(1,128)} %bitcast.11) | data formatting | bytes 1228800
  57.3 1.4 %copy.20 = f32[6,20,16]{1,2,0:T(8,128)} copy(f32[6,20,16]{1,2,0:T(8,128)} %bitcast.14) | data formatting | bytes 15360

commit v3 on v2

--- a/solution.py
+++ b/solution.py
@@ -198,6 +198,10 @@
     wc_mat,
     base,
     a_send,
+    a_pack,
+    a_in,
+    rim,
+    rim_in,
     feat_all,
     conv_all,
     taps,
@@ -213,6 +217,10 @@
     load_sem,
     a_ssem,
     a_rsem,
+    f_ssem,
+    f_rsem,
+    r_ssem,
+    r_rsem,
     m_ssem,
     m_rsem,
     sib_ssem,
@@ -287,32 +295,84 @@
         for j in range(S):
             a_send[j, r * W : (r + 1) * W, :] = padded(line[:, j * CB : (j + 1) * CB], LANES)
 
+    def pack(dst, value, main):
+        rows = value.shape[0]
+        dst[...] = value[0:main]
+        rest = rows - main
+        free = LANES - CB
+        for j in range(CB // free if rest else 0):
+            dst[j * rest : (j + 1) * rest, CB:LANES] = value[main:rows, j * free : (j + 1) * free]
+
+    def unpack(value, rows):
+        main = value.shape[0]
+        rest = rows - main
+        if not rest:
+            return (value,)
+        free = LANES - CB
+        columns = [value[j * rest : (j + 1) * rest, CB:LANES] for j in range(CB // free)]
+        return value, padded(jnp.concatenate(columns, axis=1), LANES)
+
+    def channel_stats(values):
+        total = jnp.sum(values, axis=0, keepdims=True)
+        middle = total * (1.0 / values.shape[0])
+        away = values - middle
+        return total, jnp.sum(away * away, axis=0, keepdims=True)
+
+    AM, PM, RE = dims["AM"], dims["PM"], dims["RE"]
+    AH = AM // 2
+    for j in range(S):
+        pack(a_pack.at[j], a_send[j], AM)
+
     pl.semaphore_wait(barrier, S * T * C - 1)
 
-    def a_copy(step):
+    def a_copy(step, sent):
         peer = lax.rem(s + step, S)
+        slot = s if sent else peer
+        mine = pl.ds(pl.multiple_of(c * AH, 8), AH)
         return pltpu.make_async_remote_copy(
-            src_ref=a_send.at[peer],
-            dst_ref=feat_all.at[pl.ds(pl.multiple_of(s * TILE, 8), TILE)],
+            src_ref=a_pack.at[peer, mine],
+            dst_ref=a_in.at[slot, mine],
             send_sem=a_ssem.at[peer],
-            recv_sem=a_rsem.at[s],
+            recv_sem=a_rsem.at[slot],
             device_id={"space": peer},
             device_id_type=MESH,
         )
 
-    def a_arrival(step):
-        peer = lax.rem(s + step, S)
+    def a_forward(step, half):
+        source = lax.rem(s + step, S)
+        rows = pl.ds(pl.multiple_of(half * AH, 8), AH)
         return pltpu.make_async_remote_copy(
-            src_ref=a_send.at[peer],
-            dst_ref=feat_all.at[pl.ds(pl.multiple_of(peer * TILE, 8), TILE)],
-            send_sem=a_ssem.at[peer],
-            recv_sem=a_rsem.at[peer],
-            device_id={"space": peer},
+            src_ref=a_in.at[source, rows],
+            dst_ref=a_in.at[source, rows],
+            send_sem=f_ssem.at[source],
+            recv_sem=f_rsem.at[source],
+            device_id={"chan": other},
             device_id_type=MESH,
         )
 
+    def rim_copy(dt, j, sent):
+        peer = lax.rem(t + dt, T)
+        slot_t, slot_s = (t, s) if sent else (peer, j)
+        return pltpu.make_async_remote_copy(
+            src_ref=rim.at[j],
+            dst_ref=rim_in.at[slot_t, slot_s],
+            send_sem=r_ssem.at[peer, j],
+            recv_sem=r_rsem.at[slot_t, slot_s],
+            device_id={"space": j, "tm": peer},
+            device_id_type=MESH,
+        )
+
     for step in range(1, S):
-        a_copy(step).start()
+        a_copy(step, True).start()
+    for j in range(S):
+        total, spread = channel_stats(a_send[j])
+        rim[j, 0:R, :] = a_send[j, pl.ds(0, R, stride=W), :]
+        rim[j, RE : RE + R, :] = a_send[j, pl.ds(W - 1, R, stride=W), :]
+        rim[j, 2 * RE : 2 * RE + 1, :] = total
+        rim[j, 2 * RE + 1 : 2 * RE + 2, :] = spread
+    for dt in range(1, T):
+        for j in range(S):
+            rim_copy(dt, j, True).start()
     feat_all[pl.ds(pl.multiple_of(s * TILE, 8), TILE), :] = a_send[s]
 
     def pick_block(ref):
@@ -346,12 +406,6 @@
             mat[place * LANES : place * LANES + CB, :] = value
             if gap is not None:
                 mat[place * LANES + CB : (place + 1) * LANES, :] = gap
-
-    def channel_stats(values):
-        total = jnp.sum(values, axis=0, keepdims=True)
-        middle = total * (1.0 / HM)
-        away = values - middle
-        return total, jnp.sum(away * away, axis=0, keepdims=True)
 
     edge = HR
     pad_edge = dims["EDGE"]
@@ -400,28 +454,18 @@
     left = lax.rem(t + T - 1, T)
     right = lax.rem(t + 1, T)
 
-    def activate(k, full, incoming, gain, shift):
-        parts = [channel_stats(full[h * HM : (h + 1) * HM, :]) for h in range(2)]
-        for copy in incoming:
-            copy.wait_recv()
-        for dt in range(1, T):
-            peer_t = lax.rem(t + dt, T)
-            for cc in range(C):
-                parts.append(
-                    (
-                        msg_in[k, peer_t, cc, 2 * pad_edge : 2 * pad_edge + 1, :],
-                        msg_in[k, peer_t, cc, 2 * pad_edge + 1 : 2 * pad_edge + 2, :],
-                    )
-                )
+    def activate(full, remote, rims, gain, shift):
+        parts = [channel_stats(full[h * HM : (h + 1) * HM, :]) + (HM,) for h in range(2)]
+        parts += remote
         scale = 1.0 / float(per_group * M * T)
         total = parts[0][0]
         for part in parts[1:]:
             total = total + part[0]
         center = group_sum(total) * scale
         gathered = jnp.zeros((1, LANES), F32)
-        for part_total, part_spread in parts:
-            away = part_total * (1.0 / HM) - center
-            gathered = gathered + part_spread + away * away * float(HM)
+        for part_total, part_spread, count in parts:
+            away = part_total * (1.0 / count) - center
+            gathered = gathered + part_spread + away * away * float(count)
         inverse = lax.rsqrt(group_sum(gathered) * scale + EPSILON)
         multiply = inverse
 
@@ -435,19 +479,62 @@
             taps[1, at : at + HM, :] = value
             taps[0, at + 1 : at + 1 + HM, :] = value
             taps[2, at - 1 : at - 1 + HM, :] = value
-        for h in range(C):
-            from_left = act(msg_in[k, left, h, pad_edge : pad_edge + edge, :])
-            from_right = act(msg_in[k, right, h, 0:edge, :])
-            from_left = jnp.where(t > 0, from_left, 0.0)
-            from_right = jnp.where(t < T - 1, from_right, 0.0)
-            at = W + h * HM
-            taps[0, pl.ds(at, HR, stride=W), :] = from_left
-            taps[2, pl.ds(at + W - 1, HR, stride=W), :] = from_right
+        for at, rows, raw_left, raw_right in rims:
+            from_left = jnp.where(t > 0, act(raw_left), 0.0)
+            from_right = jnp.where(t < T - 1, act(raw_right), 0.0)
+            taps[0, pl.ds(at, rows, stride=W), :] = from_left
+            taps[2, pl.ds(at + W - 1, rows, stride=W), :] = from_right
         zero = jnp.zeros((W, LANES), F32)
         tail = jnp.zeros((taps.shape[1] - W - M, LANES), F32)
         for b in range(3):
             taps[b, 0:W, :] = zero
             taps[b, W + M :, :] = tail
+
+    def first_remote():
+        parts = []
+        rims = []
+        for dt in range(1, T):
+            peer = lax.rem(t + dt, T)
+            for j in range(S):
+                rim_copy(dt, j, False).wait_recv()
+                parts.append(
+                    (
+                        rim_in[peer, j, 2 * RE : 2 * RE + 1, :],
+                        rim_in[peer, j, 2 * RE + 1 : 2 * RE + 2, :],
+                        TILE,
+                    )
+                )
+        for j in range(S):
+            rims.append(
+                (W + j * TILE, R, rim_in[left, j, RE : RE + R, :], rim_in[right, j, 0:R, :])
+            )
+        return parts, rims
+
+    def later_remote(k, incoming):
+        for copy in incoming:
+            copy.wait_recv()
+        parts = []
+        rims = []
+        for dt in range(1, T):
+            peer = lax.rem(t + dt, T)
+            for cc in range(C):
+                parts.append(
+                    (
+                        msg_in[k, peer, cc, 2 * pad_edge : 2 * pad_edge + 1, :],
+                        msg_in[k, peer, cc, 2 * pad_edge + 1 : 2 * pad_edge + 2, :],
+                        HM,
+                    )
+                )
+        for h in range(C):
+            rims.append(
+                (
+                    W + h * HM,
+                    HR,
+                    msg_in[k, left, h, pad_edge : pad_edge + edge, :],
+                    msg_in[k, right, h, 0:edge, :],
+                )
+            )
+        return parts, rims
 
     def operand(start, rows):
         pairs = []
@@ -473,7 +560,7 @@
         for h in range(2):
             part = jnp.dot(operand(h * HM, HM), mat[...], preferred_element_type=F32)
             for i in range(BH):
-                piece[k, i, h] = part[:, i * LANES : (i + 1) * LANES]
+                pack(piece.at[k, i, h], part[:, i * LANES : (i + 1) * LANES], PM)
                 block, copy = piece_copy(k, i, h)
                 away = jnp.logical_or(block != s, c != h)
 
@@ -508,10 +595,11 @@
         total = piece_in[k, 0]
         for j in range(1, S):
             total = total + piece_in[k, j]
-        start = pl.multiple_of(c * HM, 8)
-        if extra is not None:
-            total = total + extra[pl.ds(start, HM), :]
-        full[pl.ds(start, HM), :] = total
+        at = 0
+        for value in unpack(total, HM):
+            rows = pl.ds(pl.multiple_of(c * HM + at, 8), value.shape[0])
+            full[rows, :] = value if extra is None else value + extra[rows, :]
+            at += value.shape[0]
 
     def conv_drain(k):
         for h in range(2):
@@ -526,9 +614,18 @@
         load.wait()
     prepare(w1_raw, w1_mat)
     for step in range(1, S):
-        a_arrival(step).wait_recv()
-    out1, in1 = exchange(0, feat_all)
-    activate(0, feat_all, in1, pick_block(gain1), pick_block(shift1))
+        a_copy(step, False).wait_recv()
+        a_forward(step, c).start()
+    for step in range(1, S):
+        a_forward(step, other).wait_recv()
+        source = lax.rem(s + step, S)
+        at = 0
+        for value in unpack(a_in[source], TILE):
+            start = pl.multiple_of(source * TILE + at, 8)
+            feat_all[pl.ds(start, value.shape[0]), :] = value
+            at += value.shape[0]
+    parts, rims = first_remote()
+    activate(feat_all, parts, rims, pick_block(gain1), pick_block(shift1))
     conv_send(0, w1_mat)
 
     for load in loads[4:]:
@@ -582,17 +679,19 @@
     conv_receive(0, conv_all.at[0], None)
     sib1 = sibling(0, conv_all.at[0], c)
     sib1.start()
-    out2, in2 = exchange(1, conv_all.at[0])
+    out2, in2 = exchange(0, conv_all.at[0])
     sibling(0, conv_all.at[0], other).wait_recv()
-    activate(1, conv_all.at[0], in2, pick_block(gain2), pick_block(shift2))
+    parts, rims = later_remote(0, in2)
+    activate(conv_all.at[0], parts, rims, pick_block(gain2), pick_block(shift2))
     conv_send(1, w2_mat)
 
     conv_receive(1, conv_all.at[1], feat_all)
     sib2 = sibling(1, conv_all.at[1], c)
     sib2.start()
-    out3, in3 = exchange(2, conv_all.at[1])
+    out3, in3 = exchange(1, conv_all.at[1])
     sibling(1, conv_all.at[1], other).wait_recv()
-    activate(2, conv_all.at[1], in3, pick_block(gain3), pick_block(shift3))
+    parts, rims = later_remote(1, in3)
+    activate(conv_all.at[1], parts, rims, pick_block(gain3), pick_block(shift3))
 
     def lat_copy(dest_s, dest_t, dest_c, slot_s, slot_t, slot_c):
         return pltpu.make_async_remote_copy(
@@ -634,10 +733,14 @@
 
     conv_drain(0)
     conv_drain(1)
-    for copy in out1 + out2 + out3 + [sib1, sib2]:
+    for copy in out2 + out3 + [sib1, sib2]:
         copy.wait_send()
     for step in range(1, S):
-        a_copy(step).wait_send()
+        a_copy(step, True).wait_send()
+        a_forward(step, c).wait_send()
+    for dt in range(1, T):
+        for j in range(S):
+            rim_copy(dt, j, True).wait_send()
 
     for copy in lat_arrive:
         copy.wait_recv()
@@ -675,6 +778,15 @@
     return -(-value // unit) * unit
 
 
+def packed_rows(rows, width, unit):
+    free = LANES - width
+    if free <= 0 or width % free or rows % 8:
+        return rows
+    main = up(-(-rows * width // LANES), unit)
+    fits = main < rows and (rows - main) * (width // free) <= main
+    return main if fits else rows
+
+
 def plan(mesh_shape, features, noisy_latents, patch_weight):
     S, T, C = mesh_shape["space"], mesh_shape["tm"], mesh_shape["chan"]
     R, W, CH = features.shape
@@ -685,6 +797,9 @@
     dims["PR"], dims["PC"] = R // 2, W * T // 2
     dims["PP"] = up(W * T // 2, 8)
     dims["N"] = patch_weight.shape[1]
+    CB = CH // S
+    dims["AM"], dims["PM"] = packed_rows(R * W, CB, 16), packed_rows(H * W // 2, CB, 8)
+    dims["RE"] = up(R, 8)
     fits = (
         C == 2
         and T > 1
@@ -695,6 +810,8 @@
         and (R * W) % 8 == 0
         and (H * W // 2) % 8 == 0
         and H % 2 == 0
+        and dims["AM"] % 16 == 0
+        and dims["PM"] % 8 == 0
         and R * W <= LANES
         and R * Z <= LANES
         and W * T <= LANES
@@ -737,13 +854,17 @@
         pltpu.VMEM((12 * Z, N), BF16),
         pltpu.VMEM((FR, dims["PR"] * dims["PP"], N), F32),
         pltpu.VMEM((S, R * W, LANES), F32),
+        pltpu.VMEM((S, dims["AM"], LANES), F32),
+        pltpu.VMEM((S, dims["AM"], LANES), F32),
+        pltpu.VMEM((S, 2 * dims["RE"] + 8, LANES), F32),
+        pltpu.VMEM((T, S, 2 * dims["RE"] + 8, LANES), F32),
         pltpu.VMEM((M, LANES), F32),
         pltpu.VMEM((2, M, LANES), F32),
         pltpu.VMEM((3, up(M + 2 * W + LANES, 8), LANES), F32),
-        pltpu.VMEM((3, MR, LANES), F32),
-        pltpu.VMEM((3, T, C, MR, LANES), F32),
-        pltpu.VMEM((2, BH, 2, M // 2, LANES), F32),
-        pltpu.VMEM((2, S, M // 2, LANES), F32),
+        pltpu.VMEM((2, MR, LANES), F32),
+        pltpu.VMEM((2, T, C, MR, LANES), F32),
+        pltpu.VMEM((2, BH, 2, dims["PM"], LANES), F32),
+        pltpu.VMEM((2, S, dims["PM"], LANES), F32),
         pltpu.VMEM((S, Z // C, LANES), F32),
         pltpu.VMEM((T, C, S, Z // C, LANES), F32),
         pltpu.VMEM((LANES, LANES), F32),
@@ -752,8 +873,12 @@
         dma((14 + N // LANES,)),
         dma((S,)),
         dma((S,)),
-        dma((3, T, C)),
-        dma((3, T, C)),
+        dma((S,)),
+        dma((S,)),
+        dma((T, S)),
+        dma((T, S)),
+        dma((2, T, C)),
+        dma((2, T, C)),
         dma((2,)),
         dma((2,)),
         dma((2, BH, 2)),

time: 58.9 us -> 52.4 us (0.89)
  Pallas kernels: 54.7 us -> 48.1 us
    pallas_call x1, Pallas kernels: 54.7 us -> 48.1 us  [fused(): pl.pallas_call(functools.partial(fused_kernel, dims), out_shape=(jax.Shap...]
where the time goes in v3:
time: 52.4 us; the launch traced here: 52.2 us
  Pallas kernels  48.1 us (92%)
  local copies, waits for them, and re-layouts  3.37 us (6%)
  between operations  0.64 us (1%)
    pallas_call x1, Pallas kernels, fused(): pl.pallas_call(functools.partial(fused_kernel, dims), out_shape=(jax.Shap...  48.1 us
    unnamed x2, local copies, waits for them, and re-layouts  3.37 us

profile of v3, /device:TPU:0, one launch (start us, length us, event | category | flops | bytes accessed | tf_op | source)
XLA Modules:
  0.0 52.2 jit_solution(9165179600212022875)
XLA Ops:
  0.6 48.1 %fused_block.1 = (f32[3,20,1,2560]{3,2,1,0:T(1,128)}, f32[6,16,20]{2,1,0:T(8,128)}) custom-call(f32[6,20,384]{2,1,0:T(8,128)} %feat_hbm.1, f32[384]{0:T(512)} %gain1_hbm.1, f32[384]{0:T(512)} %shift1_hbm.1, f32[9,96,192]{2,1,0:T(8,128)} %bitcast.9, f32[384]{0:T(512)} %gain2_hbm.1, f32[384]{0:T(512)} %shift2_hbm.1, f32[9,96,192]{2,1,0:T(8,128)} %bitcast.10, ...), custom_call_target="tpu_custom_call" | custom-call | tf_op jit(solution)/shard_map/fused_block/pallas_call | solution.py:889
  48.8 1.9 %copy.19 = f32[1,3,20,2560]{3,0,2,1:T(1,128)} copy(f32[1,3,20,2560]{3,0,2,1:T(1,128)} %bitcast.11) | data formatting | bytes 1228800
  50.7 1.4 %copy.20 = f32[6,20,16]{1,2,0:T(8,128)} copy(f32[6,20,16]{1,2,0:T(8,128)} %bitcast.14) | data formatting | bytes 15360

commit v4 on v3

--- a/solution.py
+++ b/solution.py
@@ -157,6 +157,21 @@
     return high, (values - high.astype(F32)).astype(BF16)
 
 
+def split_columns(values):
+    high, low = split_pair(values)
+    return jnp.concatenate([high, low, high], axis=1)
+
+
+def finish_kernel(dims, patch, base, wc, latent_in, tokens, latent):
+    PC, PP, Z = dims["PC"], dims["PP"], dims["Z"]
+    for f in range(dims["FR"]):
+        lhs = split_columns(patch[f, :, 0 : 4 * Z])
+        got = base[f] + jnp.dot(lhs, wc[...], preferred_element_type=F32)
+        for p in range(dims["PR"]):
+            tokens[p, :, f, :] = got[p * PP : p * PP + PC, :]
+    latent[...] = latent_in[...]
+
+
 def fused_kernel(
     dims,
     feat_hbm,
@@ -174,7 +189,9 @@
     later_hbm,
     pw_hbm,
     patch_b_hbm,
-    tokens,
+    patch_out,
+    base_out,
+    wc_out,
     latent,
     feat,
     gain1,
@@ -194,6 +211,7 @@
     w1_mat,
     w2_mat,
     wh_mat,
+    mixed,
     wn_mat,
     wc_mat,
     base,
@@ -631,9 +649,11 @@
     for load in loads[4:]:
         load.wait()
     prepare(w2_raw, w2_mat)
-    for tap in range(9):
-        high, low = split_pair(padded(head_w[tap], LANES))
-        for place, value in ((2 * tap, high), (2 * tap + 1, high), (18 + tap, low)):
+    blank = jnp.zeros((LANES - 3 * ZH, LANES), F32)
+    for b in range(3):
+        rows = [padded(head_w[a * 3 + b], LANES) for a in range(3)] + [blank]
+        high, low = split_pair(jnp.concatenate(rows, axis=0))
+        for place, value in ((3 * b, high), (3 * b + 1, high), (3 * b + 2, low)):
             wh_mat[:, place * LANES : (place + 1) * LANES] = value
     for first, mat in ((0, wn_mat), (4 * (Z + 4), wc_mat)):
         for b in range(2):
@@ -658,7 +678,7 @@
     cells[...] = jnp.zeros(cells.shape, F32)
     patch[...] = jnp.zeros(patch.shape, F32)
 
-    def patches_of_cells():
+    def build_patches():
         turned[...] = cells[...].T
         for b in range(2):
             picked = turned[pl.ds(b, PC, stride=2), :]
@@ -666,15 +686,21 @@
                 patch[p * PP : p * PP + PC, b * 2 * Z : (b + 1) * 2 * Z] = picked[
                     :, p * 2 * Z : (p + 1) * 2 * Z
                 ]
-        high, low = split_pair(patch[:, 0 : 4 * Z])
-        return jnp.concatenate([high, low, high], axis=1)
 
     for f in range(FR):
         for i in range(R):
             cells[i * Z : (i + 1) * Z, 0:FULLW] = noisy[f, i]
-        got = jnp.dot(patches_of_cells(), wn_mat[...], preferred_element_type=F32)
+        build_patches()
+        got = jnp.dot(split_columns(patch[:, 0 : 4 * Z]), wn_mat[...], preferred_element_type=F32)
         opening = (t * FR + f) == 0
         base[f] = got + patch_b[...].reshape(1, -1) + jnp.where(opening, mark_sum, 0.0)
+
+    stores = [
+        pltpu.make_async_copy(base, base_out, load_sem.at[len(early) + strips]),
+        pltpu.make_async_copy(wc_mat, wc_out, load_sem.at[len(early) + strips + 1]),
+    ]
+    for store in stores:
+        store.start()
 
     conv_receive(0, conv_all.at[0], None)
     sib1 = sibling(0, conv_all.at[0], c)
@@ -708,14 +734,22 @@
         jnp.int32, (ZH, ZH), 1
     )
     bias = jnp.sum(jnp.where(diagonal & (s == 0), bias_row, 0.0), axis=1, keepdims=True)
+    columns = []
+    for b in range(3):
+        high, low = split_pair(taps[b, 0 : mixed.shape[0], :])
+        columns += [high, low, high]
+    mixed[...] = lax.dot_general(
+        jnp.concatenate(columns, axis=1),
+        wh_mat[...],
+        (((1,), (1,)), ((), ())),
+        preferred_element_type=F32,
+    )
     for j in range(S):
-        part = lax.dot_general(
-            wh_mat[...],
-            operand(j * TILE, LANES),
-            (((1,), (1,)), ((), ())),
-            preferred_element_type=F32,
-        )
-        lat_send[j] = part + bias
+        shifted = [mixed[j * TILE + a * W : j * TILE + a * W + LANES, :] for a in range(3)]
+        joined = jnp.where(
+            col_id < ZH, shifted[0], jnp.where(col_id < 2 * ZH, shifted[1], shifted[2])
+        ).T
+        lat_send[j] = joined[0:ZH] + joined[ZH : 2 * ZH] + joined[2 * ZH : 3 * ZH] + bias
     lat_in[t, c, s] = lat_send[s]
     lat_out = []
     lat_arrive = []
@@ -767,9 +801,10 @@
         for i in range(R):
             rows = slice(i * Z, (i + 1) * Z)
             cells[rows, 0:FULLW] = jnp.where(opening, cells[rows, 0:FULLW], later[f, i])
-        got = base[f] + jnp.dot(patches_of_cells(), wc_mat[...], preferred_element_type=F32)
-        for p in range(PR):
-            tokens[p, :, f, :] = got[p * PP : p * PP + PC, :]
+        build_patches()
+        patch_out[f] = patch[...]
+    for store in stores:
+        store.wait()
     for copy in lat_out:
         copy.wait_send()
 
@@ -849,7 +884,8 @@
         pltpu.VMEM((N // LANES, pw.shape[0], LANES), F32),
         big(BH * LANES),
         big(BH * LANES),
-        pltpu.VMEM((Z // C, 27 * LANES), BF16),
+        pltpu.VMEM((LANES, 9 * LANES), BF16),
+        pltpu.VMEM((up((S - 1) * R * W + 2 * W + LANES, 16), LANES), F32),
         pltpu.VMEM((12 * Z, N), BF16),
         pltpu.VMEM((12 * Z, N), BF16),
         pltpu.VMEM((FR, dims["PR"] * dims["PP"], N), F32),
@@ -870,7 +906,7 @@
         pltpu.VMEM((LANES, LANES), F32),
         pltpu.VMEM((LANES, LANES), F32),
         pltpu.VMEM((dims["PR"] * dims["PP"], LANES), F32),
-        dma((14 + N // LANES,)),
+        dma((16 + N // LANES,)),
         dma((S,)),
         dma((S,)),
         dma((S,)),
@@ -886,20 +922,42 @@
         dma((T, C, S)),
         dma((T, C, S)),
     ]
-    tokens, latent = pl.pallas_call(
+    PR, PC, PP = dims["PR"], dims["PC"], dims["PP"]
+    far = pl.BlockSpec(memory_space=pl.ANY)
+    patch, base, wc, latent = pl.pallas_call(
         functools.partial(fused_kernel, dims),
         out_shape=(
-            jax.ShapeDtypeStruct((dims["PR"], dims["PC"], FR, N), F32),
+            jax.ShapeDtypeStruct((FR, PR * PP, LANES), F32),
+            jax.ShapeDtypeStruct((FR, PR * PP, N), F32),
+            jax.ShapeDtypeStruct((12 * Z, N), BF16),
             jax.ShapeDtypeStruct((R, Z, W), F32),
         ),
         in_specs=in_specs,
-        out_specs=(vmem, vmem),
+        out_specs=(vmem, far, far, vmem),
         scratch_shapes=scratch,
         compiler_params=pltpu.CompilerParams(
             collective_id=0, has_side_effects=True, vmem_limit_bytes=60 * 2**20
         ),
         name="fused_block",
     )(*operands)
+    NB = N // 4 if N % (4 * LANES) == 0 else N
+    whole = lambda shape: pl.BlockSpec(shape, lambda n: (0,) * len(shape))
+    tokens, latent = pl.pallas_call(
+        functools.partial(finish_kernel, dims),
+        grid=(N // NB,),
+        out_shape=(
+            jax.ShapeDtypeStruct((PR, PC, FR, N), F32),
+            jax.ShapeDtypeStruct((R, Z, W), F32),
+        ),
+        in_specs=[
+            whole((FR, PR * PP, LANES)),
+            pl.BlockSpec((FR, PR * PP, NB), lambda n: (0, 0, n)),
+            pl.BlockSpec((12 * Z, NB), lambda n: (0, n)),
+            whole((R, Z, W)),
+        ],
+        out_specs=(pl.BlockSpec((PR, PC, FR, NB), lambda n: (0, 0, 0, n)), whole((R, Z, W))),
+        name="finish_tokens",
+    )(patch, base, wc, latent)
     return jnp.transpose(tokens, (2, 0, 1, 3)), jnp.transpose(latent, (0, 2, 1))
 
 

time: 52.4 us -> 51.9 us (level)
  local copies, waits for them, and re-layouts: 3.37 us -> 0 us
  Pallas kernels: 48.1 us -> 51.1 us
    pallas_call x0 -> x1, Pallas kernels: none -> 3.96 us  [fused(): pl.pallas_call(functools.partial(finish_kernel, dims), grid=(N // NB,), o...]
    unnamed x2 -> x0, local copies, waits for them, and re-layouts: 3.37 us -> none
    pallas_call x1, Pallas kernels: 48.1 us -> 47.1 us  [fused(): pl.pallas_call(functools.partial(fused_kernel, dims), out_shape=(jax.Shap...]
where the time goes in v4:
time: 51.9 us; the launch traced here: 51.7 us
  Pallas kernels  51.1 us (98%)
  between operations  0.64 us (1%)
    pallas_call x1, Pallas kernels, fused(): pl.pallas_call(functools.partial(fused_kernel, dims), out_shape=(jax.Shap...  47.1 us
    pallas_call x1, Pallas kernels, fused(): pl.pallas_call(functools.partial(finish_kernel, dims), grid=(N // NB,), o...  3.96 us

profile of v4, /device:TPU:0, one launch (start us, length us, event | category | flops | bytes accessed | tf_op | source)
XLA Modules:
  0.0 51.7 jit_solution(2974381320475349495)
XLA Ops:
  0.6 47.1 %fused_block.1 = (f32[1,72,128]{2,1,0:T(8,128)}, f32[1,72,2560]{2,1,0:T(8,128)}, bf16[192,2560]{1,0:T(8,128)(2,1)}, f32[6,16,20]{2,1,0:T(8,128)}) custom-call(f32[6,20,384]{2,1,0:T(8,128)} %feat_hbm.1, f32[384]{0:T(512)} %gain1_hbm.1, f32[384]{0:T(512)} %shift1_hbm.1, f32[9,96,192]{2,1,0:T(8,128)} %bitcast.9, f32[384]{0:T(512)} %gain2_hbm.1, f32[384]{0:T(512)} %shift2_hbm.1, ...), custom_call_target="tpu_custom_call" | custom-call | tf_op jit(solution)/shard_map/fused_block/pallas_call | solution.py:927
  47.8 4.0 %finish_tokens.1 = (f32[3,20,1,2560]{3,2,1,0:T(1,128)}, f32[6,16,20]{2,1,0:T(8,128)}) custom-call(f32[1,72,128]{2,1,0:T(8,128)} %get-tuple-element.8.patch, f32[1,72,2560]{2,1,0:T(8,128)} %get-tuple-element.9.base, bf16[192,2560]{1,0:T(8,128)(2,1)} %get-tuple-element.10.wc, f32[6,16,20]{2,1,0:T(8,128)} %get-tuple-element.11.latent_in), custom_call_target="tpu_custom_call" | custom-call | tf_op jit(solution)/shard_map/finish_tokens/pallas_call | solution.py:945
